TPU v7x, 256 devices: a whole 4x4x8 slice. The times are simulated.
256 devices in a mesh: obs: 4 (over x), pix: 16 (over z, core), chan: 4 (over y).
Axes of the slice: x: 4, y: 4, z: 8, core: 2. Of those that a mesh axis runs over, the one named last changes fastest.
Arguments:
- spectra: bfloat16 [131072, 4608], P(('obs', 'pix'), 'chan'), may hold values from -6 to 6
- enc_weight: bfloat16 [4608, 256], P('chan'), may hold values from -0.09375 to 0.09375
- pix_tile: int32 [131072, 1], P(('obs', 'pix')), may hold values from 0 to 15; in each aligned block of 512 rows (0 to 511, 512 to 1023, ...) at most 64 rows name the same one
- pix_local: int32 [131072], P(('obs', 'pix')), may hold values from 0 to 4095
- foot_weight: float32 [131072], P(('obs', 'pix')), may hold values from 0.001 to 0.01
- cotangent: bfloat16 [65536, 256], P('pix'), may hold values from -6 to 6
- adjoint: int32 [8, 65536], P(None, 'pix'), may hold values from 0 to 65535, as said below
- mixing: float32 [8, 256], replicated, may hold values from -2 to 2
Outputs:
- grad_enc: float32 [4608, 256], P('chan')
Inputs may be any that keep to these rules, and one draw needn't show every extreme that they name: `pix_tile`: in each aligned block of 512 rows no tile is named by more than 64 rows, a bound that some block reaches. `adjoint`: every entry is a pixel at most 128 away in index from its column's pixel; in every column the first entry is exactly 128 away.
All inputs are finite; a program needn't handle non-finite values.
Results may differ from a plain program's by a relative error of at most 0.006.
Values may be sent and summed in bfloat16 or wider, within the bound.
A program may use at most 128 MiB of HBM per device.

v0:
```python
import jax
import jax.numpy as jnp
from jax import lax
from jax.sharding import Mesh
from jax.sharding import PartitionSpec as P

NEIGH = 8
HALO = 128
PIX = ("pix_0", "pix_1")
OBS_PIX = ("obs", "pix_0", "pix_1")


def extended(value, sides, width):
    for axis, dim in sides:
        size, length = (lax.axis_size(axis), value.shape[dim])
        up = [(i, (i + 1) % size) for i in range(size - 1)]
        down = [(j, i) for i, j in up]
        last = lax.slice_in_dim(value, length - width, length, axis=dim)
        first = lax.slice_in_dim(value, 0, width, axis=dim)
        before = lax.ppermute(last, axis, up)
        after = lax.ppermute(first, axis, down)
        value = jnp.concatenate([before, value, after], axis=dim)
    return value


def in_blocks(value, dim, length):
    before, after = (value.shape[:dim], value.shape[dim + 1 :])
    return jnp.moveaxis(value.reshape(*before, length, -1, *after), dim, 0)


def summed_on_arrival(value, axis, dim):
    pieces = in_blocks(value, dim, lax.axis_size(axis))
    arrived = lax.all_to_all(pieces, axis, split_axis=0, concat_axis=0, tiled=True)
    return arrived.astype(jnp.float32).sum(axis=0)


def laid_out(pieces, dim):
    pieces = jnp.moveaxis(pieces, 0, dim)
    dims = pieces.shape
    return pieces.reshape(*dims[:dim], dims[dim] * dims[dim + 1], *dims[dim + 2 :])


def copy_for_each(value, axis):
    length = lax.axis_size(axis)
    return lax.all_to_all(
        jnp.broadcast_to(value[None], (length, *value.shape)), axis, 0, 0, tiled=True
    )


def collect(value, axis, dim):
    return laid_out(copy_for_each(value, axis), dim)


def rows_for(lines, length):
    spare = -lines.shape[0] % length
    if not spare:
        return lines
    return jnp.concatenate([lines, jnp.zeros((spare, *lines.shape[1:]), lines.dtype)])


def gather_axes(value, axes, dim):
    far, near = axes
    first = copy_for_each(value, far)
    pieces = jnp.swapaxes(copy_for_each(first, near), 0, 1)
    return laid_out(pieces.reshape(-1, *value.shape), dim)


def sum_at_owner(value, axis, dim):
    pieces = in_blocks(value, dim, lax.axis_size(axis))
    arrived = lax.all_to_all(pieces, axis, split_axis=0, concat_axis=0, tiled=True)
    return arrived.sum(axis=0)


def sum_in_two_steps(value, axes, dim):
    far, near = axes
    own = sum_at_owner(in_blocks(value, dim, lax.axis_size(far)), near, dim + 1)
    return jnp.sum(lax.all_to_all(own, far, 0, 0, tiled=True), axis=0)


def total_of(value, axes):
    lines = value.reshape(-1, value.shape[-1])
    padded = rows_for(lines, lax.axis_size(axes[0]) * lax.axis_size(axes[1]))
    whole = gather_axes(sum_in_two_steps(padded, axes, 0), axes, 0)
    return lax.slice_in_dim(whole, 0, len(lines)).reshape(value.shape)


def fetch_rows(pixel_grad, tile_ids, local_ids, capacity):
    tile_count = lax.axis_size(PIX)
    feature_count = pixel_grad.shape[1]
    onehot = (tile_ids[:, None] == jnp.arange(tile_count, dtype=jnp.int32)[None, :]).astype(
        jnp.int32
    )
    place_rank = jnp.sum((jnp.cumsum(onehot, axis=0) - 1) * onehot, axis=1)
    slot_index = tile_ids * capacity + place_rank
    outgoing = jnp.full((tile_count * capacity,), -1, jnp.int32).at[slot_index].set(local_ids)
    outgoing = outgoing.reshape(tile_count, capacity)
    requested = lax.all_to_all(outgoing, PIX, split_axis=0, concat_axis=0, tiled=True)
    usable = requested >= 0
    fetched = jnp.take(pixel_grad, jnp.where(usable, requested, 0), axis=0)
    fetched = jnp.where(usable[..., None], fetched, jnp.zeros_like(fetched))
    answers = lax.all_to_all(fetched, PIX, split_axis=0, concat_axis=0, tiled=True)
    return jnp.take(answers.reshape(tile_count * capacity, feature_count), slot_index, axis=0)


def pre_gradient(pre, fetched, weights):
    sigma = jax.nn.sigmoid(pre)
    deriv = sigma * (1.0 + pre * (1.0 - sigma))
    return (weights[:, None] * deriv * fetched.astype(jnp.float32)).astype(jnp.bfloat16)


def shards(spectra, enc_weight, pix_tile, pix_local, foot_weight, cotangent, adjoint, mixing):
    tile_count = lax.axis_size(PIX)
    groups = lax.axis_size("chan")
    tile_rows = cotangent.shape[0]
    feature_count = cotangent.shape[1]
    padded = extended(cotangent, ((PIX, 0),), HALO)
    block_count = tile_rows // HALO
    stacked = padded.reshape(block_count + 2, HALO, feature_count)
    windows = jnp.concatenate(
        (stacked[:block_count], stacked[1 : block_count + 1], stacked[2 : block_count + 2]), axis=1
    )
    anchor = lax.axis_index(PIX) * tile_rows - HALO
    block_start = (jnp.arange(block_count, dtype=jnp.int32) * HALO)[:, None]
    columns = jnp.arange(3 * HALO, dtype=jnp.int32)[None, None, :]
    summed = cotangent.astype(jnp.float32)
    for neighbor in range(NEIGH):
        within = (adjoint[neighbor] - anchor).reshape(block_count, HALO) - block_start
        selector = (within[:, :, None] == columns).astype(jnp.bfloat16)
        picked = jnp.einsum("bij,bje->bie", selector, windows, preferred_element_type=jnp.float32)
        summed = summed + picked.reshape(tile_rows, feature_count) * mixing[neighbor]
    pixel_grad = summed.astype(jnp.bfloat16)
    all_rows = spectra.shape[0]
    quarter = all_rows // groups
    capacity_part = 2 * quarter // tile_count
    pre = summed_on_arrival(
        jnp.dot(spectra, enc_weight, preferred_element_type=jnp.float32).astype(jnp.bfloat16),
        "chan",
        0,
    )
    first_row = lax.axis_index("chan") * quarter
    tile_ids = lax.dynamic_slice_in_dim(pix_tile[:, 0], first_row, quarter, 0)
    local_ids = lax.dynamic_slice_in_dim(pix_local, first_row, quarter, 0)
    weights = lax.dynamic_slice_in_dim(foot_weight, first_row, quarter, 0)
    fetched = fetch_rows(pixel_grad, tile_ids, local_ids, capacity_part)
    grad_part = pre_gradient(pre, fetched, weights)
    local_grad = lax.dot_general(
        spectra,
        collect(grad_part, "chan", 0),
        (((0,), (0,)), ((), ())),
        preferred_element_type=jnp.float32,
    )
    return total_of(local_grad, (("obs", "pix_0"), "pix_1"))


def solution(mesh):
    finer = Mesh(
        mesh.devices.reshape(mesh.shape["obs"], 8, 2, mesh.shape["chan"]),
        ("obs", "pix_0", "pix_1", "chan"),
    )
    placed = (
        P(OBS_PIX, "chan"),
        P("chan", None),
        P(OBS_PIX, None),
        P(OBS_PIX),
        P(OBS_PIX),
        P(PIX, None),
        P(None, PIX),
        P(),
    )
    return jax.shard_map(
        shards, mesh=finer, in_specs=placed, out_specs=P("chan", None), check_vma=False
    )
```

profile of v0, /device:TPU:1, one launch (start us, length us, event | category | flops | bytes accessed | tf_op | source)
XLA Modules:
  0.0 198.4 jit_solution(14028622263812513559)
XLA Ops:
  0.9 4.9 %collective-permute-start = (bf16[128,256]{1,0:T(8,128)(2,1)S(1)}, bf16[128,256]{1,0:T(8,128)(2,1)S(1)}, u32[]{:S(2)}, u32[]{:S(2)}) collective-permute-start(bf16[128,256]{1,0:T(8,128)(2,1)S(1)} %get-tuple-element.9), channel_id=1, source_target_pairs={{0,4},{4,8},{8,12},{12,16},{16,20},{20,24},{24,28},{28,32},{32,36}... | collective-permute-start | bytes 196616 | tf_op jit(solution)/shard_map/ppermute | solution.py:20
  11.5 2.4 %scatter_custom_fusion = s32[1024]{0:T(1024)S(1)} fusion(s32[512]{0:T(512)S(1)} %bitcast.144, s32[512]{0:T(512)S(1)} %dynamic_slice.11, s32[]{:T(128)} %constant.37.clone.1), kind=kCustom, calls=%fused_computation.85 | custom fusion | bytes 4100 | tf_op jit(solution)/shard_map/scatter | solution.py:95
  14.6 9.9 %all-to-all-start.1 = ((s32[16,1,64]{2,1,0:T(1,128)}), s32[16,1,64]{2,1,0:T(1,128)S(1)}, u32[]{:S(2)}, u32[]{:S(2)}) async-start(s32[16,1,64]{2,1,0:T(1,128)} %all_to_all.32), calls=%async_computation.1 | async-start | bytes 16384 | tf_op jit(solution)/shard_map/all_to_all | solution.py:97
  26.5 5.0 %convolution_convert_fusion = bf16[2048,256]{1,0:T(8,128)(2,1)} fusion(bf16[2048,1152]{1,0:T(8,128)(2,1)} %param.8, bf16[1152,256]{1,0:T(8,128)(2,1)S(1)} %copy-done), kind=kOutput, calls=%fused_computation.46 | convolution fusion | flops 1208483840 | bytes 6356992 | tf_op jit(solution)/shard_map/dot_general | solution.py:136
  31.6 4.3 %all-to-all-start = ((bf16[4,512,256]{2,1,0:T(8,128)(2,1)}), bf16[4,512,256]{2,1,0:T(8,128)(2,1)}, u32[]{:S(2)}, u32[]{:S(2)}) async-start(bf16[4,512,256]{2,1,0:T(8,128)(2,1)} %bitcast.130), calls=%async_computation | async-start | bytes 2097152 | tf_op jit(solution)/shard_map/all_to_all | solution.py:33
  36.3 2.9 %fusion = f32[32,128,256]{2,1,0:T(8,128)S(1)} fusion(s32[32,128]{1,0:T(8,128)S(1)} %get-tuple-element.29, bf16[32,128,256]{2,1,0:T(8,128)(2,1)S(1)} %bitcast.121, bf16[32,128,256]{2,1,0:T(8,128)(2,1)S(1)} %bitcast.103, bf16[32,128,256]{2,1,0:T(8,128)(2,1)S(1)} %bitcast.113), kind=kOutput, calls=%fused_computation.12 | convolution fusion | flops 825753600 | bytes 10502144 | tf_op jit(solution)/shard_map/bij,bje->bie/dot_general | solution.py:129
  39.2 2.9 %fusion.1 = f32[32,128,256]{2,1,0:T(8,128)S(1)} fusion(s32[32,128]{1,0:T(8,128)S(1)} %get-tuple-element.30, bf16[32,128,256]{2,1,0:T(8,128)(2,1)S(1)} %bitcast.122, bf16[32,128,256]{2,1,0:T(8,128)(2,1)S(1)} %bitcast.104, bf16[32,128,256]{2,1,0:T(8,128)(2,1)S(1)} %bitcast.114), kind=kOutput, calls=%fused_computation.13 | convolution fusion | flops 825753600 | bytes 10502144 | tf_op jit(solution)/shard_map/bij,bje->bie/dot_general | solution.py:129
  42.0 3.5 %fusion.2 = f32[32,128,256]{2,1,0:T(8,128)} fusion(s32[32,128]{1,0:T(8,128)S(1)} %get-tuple-element.31, bf16[32,128,256]{2,1,0:T(8,128)(2,1)S(1)} %bitcast.123, bf16[32,128,256]{2,1,0:T(8,128)(2,1)S(1)} %bitcast.105, bf16[32,128,256]{2,1,0:T(8,128)(2,1)S(1)} %bitcast.115), kind=kOutput, calls=%fused_computation.14 | convolution fusion | flops 825753600 | bytes 10502144 | tf_op jit(solution)/shard_map/bij,bje->bie/dot_general | solution.py:129
  45.5 3.5 %fusion.3 = f32[32,128,256]{2,1,0:T(8,128)} fusion(s32[32,128]{1,0:T(8,128)S(1)} %get-tuple-element.32, bf16[32,128,256]{2,1,0:T(8,128)(2,1)S(1)} %bitcast.124, bf16[32,128,256]{2,1,0:T(8,128)(2,1)S(1)} %bitcast.106, bf16[32,128,256]{2,1,0:T(8,128)(2,1)S(1)} %bitcast.116), kind=kOutput, calls=%fused_computation.15 | convolution fusion | flops 825753600 | bytes 10502144 | tf_op jit(solution)/shard_map/bij,bje->bie/dot_general | solution.py:129
  49.0 3.5 %fusion.4 = f32[32,128,256]{2,1,0:T(8,128)} fusion(s32[32,128]{1,0:T(8,128)S(1)} %get-tuple-element.33, bf16[32,128,256]{2,1,0:T(8,128)(2,1)S(1)} %bitcast.125, bf16[32,128,256]{2,1,0:T(8,128)(2,1)S(1)} %bitcast.107, bf16[32,128,256]{2,1,0:T(8,128)(2,1)S(1)} %bitcast.117), kind=kOutput, calls=%fused_computation.16 | convolution fusion | flops 825753600 | bytes 10502144 | tf_op jit(solution)/shard_map/bij,bje->bie/dot_general | solution.py:129
  52.5 3.5 %fusion.5 = f32[32,128,256]{2,1,0:T(8,128)} fusion(s32[32,128]{1,0:T(8,128)S(1)} %get-tuple-element.34, bf16[32,128,256]{2,1,0:T(8,128)(2,1)S(1)} %bitcast.126, bf16[32,128,256]{2,1,0:T(8,128)(2,1)S(1)} %bitcast.108, bf16[32,128,256]{2,1,0:T(8,128)(2,1)S(1)} %bitcast.118), kind=kOutput, calls=%fused_computation.17 | convolution fusion | flops 825753600 | bytes 10502144 | tf_op jit(solution)/shard_map/bij,bje->bie/dot_general | solution.py:129
  56.0 3.5 %fusion.6 = f32[32,128,256]{2,1,0:T(8,128)} fusion(s32[32,128]{1,0:T(8,128)S(1)} %get-tuple-element.35, bf16[32,128,256]{2,1,0:T(8,128)(2,1)S(1)} %bitcast.127, bf16[32,128,256]{2,1,0:T(8,128)(2,1)S(1)} %bitcast.109, bf16[32,128,256]{2,1,0:T(8,128)(2,1)S(1)} %bitcast.119), kind=kOutput, calls=%fused_computation.18 | convolution fusion | flops 825753600 | bytes 10502144 | tf_op jit(solution)/shard_map/bij,bje->bie/dot_general | solution.py:129
  59.5 3.5 %fusion.7 = f32[32,128,256]{2,1,0:T(8,128)} fusion(s32[32,128]{1,0:T(8,128)S(1)} %get-tuple-element.36, bf16[32,128,256]{2,1,0:T(8,128)(2,1)S(1)} %bitcast.128, bf16[32,128,256]{2,1,0:T(8,128)(2,1)S(1)} %bitcast.110, bf16[32,128,256]{2,1,0:T(8,128)(2,1)S(1)} %bitcast.120), kind=kOutput, calls=%fused_computation.19 | convolution fusion | flops 825753600 | bytes 10502144 | tf_op jit(solution)/shard_map/bij,bje->bie/dot_general | solution.py:129
  62.9 9.6 %fusion.9 = bf16[4096,256]{1,0:T(8,128)(2,1)S(1)} fusion(f32[32,128,256]{2,1,0:T(8,128)} %fusion.7, f32[32,128,256]{2,1,0:T(8,128)} %fusion.6, f32[32,128,256]{2,1,0:T(8,128)} %fusion.5, f32[32,128,256]{2,1,0:T(8,128)} %fusion.4, f32[32,128,256]{2,1,0:T(8,128)} %fusion.3, f32[32,128,256]{2,1,0:T(8,128)} %fusion.2, f32[32,128,256]{2,1,0:T(8,128)S(1)} %fusion.1, ...), kind=kLoop, calls=%fused_computation.22 | loop fusion | flops 18874368 | bytes 37756928 | tf_op jit(solution)/shard_map/convert_element_type | solution.py:131
  72.6 3.9 %gather_fusion = bf16[1024,256]{1,0:T(8,128)(2,1)S(1)} fusion(bf16[4096,256]{1,0:T(8,128)(2,1)S(1)} %fusion.9, s32[1024]{0:T(1024)S(1)} %broadcast_clamp_fusion), kind=kCustom, calls=%fused_computation | custom fusion | bytes 1052672 | tf_op jit(solution)/shard_map/jit(_take)/gather | solution.py:99
  77.7 7.5 %all-to-all-start.2 = ((bf16[16,64,256]{2,1,0:T(8,128)(2,1)}), bf16[16,64,256]{2,1,0:T(8,128)(2,1)S(1)}, u32[]{:S(2)}, u32[]{:S(2)}) async-start(bf16[16,64,256]{2,1,0:T(8,128)(2,1)} %select_select_fusion), calls=%async_computation.2 | async-start | bytes 1048576 | tf_op jit(solution)/shard_map/all_to_all | solution.py:101
  87.3 15.0 %all-to-all-done.2 = bf16[16,64,256]{2,1,0:T(8,128)(2,1)S(1)} async-done(((bf16[16,64,256]{2,1,0:T(8,128)(2,1)}), bf16[16,64,256]{2,1,0:T(8,128)(2,1)S(1)}, u32[]{:S(2)}, u32[]{:S(2)}) %all-to-all-start.2) | async-done | bytes 524320 | tf_op jit(solution)/shard_map/all_to_all | solution.py:101
  102.3 1.9 gather_fusion.1
  104.7 19.2 %all_to_all.50 = bf16[4,512,256]{2,1,0:T(8,128)(2,1)S(1)} all-to-all(bf16[4,512,256]{2,1,0:T(8,128)(2,1)S(1)} %broadcast_in_dim.79), channel_id=1, replica_groups=mesh['obs'=4,'pix_0'=8,'pix_1'=2,'chan'=4] {'chan'}, dimensions={0} | all-to-all | bytes 2097152 | tf_op jit(solution)/shard_map/all_to_all | solution.py:45
  123.9 3.9 %convolution_bitcast_fusion = f32[1152,256]{0,1:T(8,128)S(1)} fusion(bf16[2048,256]{1,0:T(8,128)(2,1)S(1)} %bitcast.131, bf16[2048,1152]{1,0:T(8,128)(2,1)} %param.8), kind=kOutput, calls=%fused_computation.45 | convolution fusion | flops 1207959552 | bytes 6946816 | tf_op jit(solution)/shard_map/dot_general | solution.py:146
  129.0 4.6 %all_to_all.51 = f32[2,32,18,256]{3,1,2,0:T(8,128)S(1)} all-to-all(f32[2,32,18,256]{3,1,2,0:T(8,128)S(1)} %copy.22), channel_id=1, replica_groups=mesh['obs'=4,'pix_0'=8,'pix_1'=2,'chan'=4] {'pix_1'}, dimensions={0} | all-to-all | bytes 2359296 | tf_op jit(solution)/shard_map/all_to_all | solution.py:70
  134.1 24.6 %all_to_all.52 = f32[32,18,256]{2,1,0:T(8,128)S(1)} all-to-all(f32[32,18,256]{2,1,0:T(8,128)S(1)} %copy.23), channel_id=1, replica_groups=mesh['obs'=4,'pix_0'=8,'pix_1'=2,'chan'=4] {'obs','pix_0'}, dimensions={0} | all-to-all | bytes 1179648 | tf_op jit(solution)/shard_map/all_to_all | solution.py:77
  158.8 28.5 %all_to_all.53 = f32[32,18,256]{2,1,0:T(8,128)S(1)} all-to-all(f32[32,18,256]{2,1,0:T(8,128)S(1)} %broadcast_in_dim.80), channel_id=1, replica_groups=mesh['obs'=4,'pix_0'=8,'pix_1'=2,'chan'=4] {'obs','pix_0'}, dimensions={0} | all-to-all | bytes 1179648 | tf_op jit(solution)/shard_map/all_to_all | solution.py:45
  187.6 9.0 %all_to_all.54 = f32[2,32,18,256]{3,1,2,0:T(8,128)S(1)} all-to-all(f32[2,32,18,256]{3,1,2,0:T(8,128)S(1)} %broadcast_in_dim.81), channel_id=1, replica_groups=mesh['obs'=4,'pix_0'=8,'pix_1'=2,'chan'=4] {'pix_1'}, dimensions={0} | all-to-all | bytes 2359296 | tf_op jit(solution)/shard_map/all_to_all | solution.py:45
  (52 shorter events, 17.3 us)
Async XLA Ops:
  0.0 26.5 %copy-start = (bf16[1152,256]{1,0:T(8,128)(2,1)S(1)}, bf16[1152,256]{1,0:T(8,128)(2,1)}, u32[]{:S(2)}) copy-start(bf16[1152,256]{1,0:T(8,128)(2,1)} %param.9) | copy-start | bytes 1769476
  0.9 35.0 %collective-permute-start = (bf16[128,256]{1,0:T(8,128)(2,1)S(1)}, bf16[128,256]{1,0:T(8,128)(2,1)S(1)}, u32[]{:S(2)}, u32[]{:S(2)}) collective-permute-start(bf16[128,256]{1,0:T(8,128)(2,1)S(1)} %get-tuple-element.9), channel_id=1, source_target_pairs={{0,4},{4,8},{8,12},{12,16},{16,20},{20,24},{24,28},{28,32},{32,36}... | collective-permute-start | bytes 196616 | tf_op jit(solution)/shard_map/ppermute | solution.py:20
  5.9 30.1 %collective-permute-start.1 = (bf16[128,256]{1,0:T(8,128)(2,1)S(1)}, bf16[128,256]{1,0:T(8,128)(2,1)S(1)}, u32[]{:S(2)}, u32[]{:S(2)}) collective-permute-start(bf16[128,256]{1,0:T(8,128)(2,1)S(1)} %get-tuple-element.10), channel_id=1, source_target_pairs={{4,0},{8,4},{12,8},{16,12},{20,16},{24,20},{28,24},{32,28},{36,32}... | collective-permute-start | bytes 196616 | tf_op jit(solution)/shard_map/ppermute | solution.py:21
  14.6 17.0 %all-to-all-start.1 = ((s32[16,1,64]{2,1,0:T(1,128)}), s32[16,1,64]{2,1,0:T(1,128)S(1)}, u32[]{:S(2)}, u32[]{:S(2)}) async-start(s32[16,1,64]{2,1,0:T(1,128)} %all_to_all.32), calls=%async_computation.1 | async-start | bytes 16384 | tf_op jit(solution)/shard_map/all_to_all | solution.py:97
  26.5 5.1 %copy-start.4 = (f32[8,256]{1,0:T(8,128)S(1)}, f32[8,256]{1,0:T(8,128)}, u32[]{:S(2)}) copy-start(f32[8,256]{1,0:T(8,128)} %param.15) | copy-start | bytes 24580
  26.5 9.5 %copy-start.2 = (bf16[4096,256]{1,0:T(8,128)(2,1)S(1)}, bf16[4096,256]{1,0:T(8,128)(2,1)}, u32[]{:S(2)}) copy-start(bf16[4096,256]{1,0:T(8,128)(2,1)} %param.13) | copy-start | bytes 6291460
  31.6 46.1 %all-to-all-start = ((bf16[4,512,256]{2,1,0:T(8,128)(2,1)}), bf16[4,512,256]{2,1,0:T(8,128)(2,1)}, u32[]{:S(2)}, u32[]{:S(2)}) async-start(bf16[4,512,256]{2,1,0:T(8,128)(2,1)} %bitcast.130), calls=%async_computation | async-start | bytes 2097152 | tf_op jit(solution)/shard_map/all_to_all | solution.py:33
  59.5 3.5 %copy-start.3 = (bf16[4096,256]{1,0:T(8,128)(2,1)S(1)}, bf16[4096,256]{1,0:T(8,128)(2,1)}, u32[]{:S(2)}) copy-start(bf16[4096,256]{1,0:T(8,128)(2,1)} %param.13) | copy-start | bytes 6291460
  77.7 24.7 %all-to-all-start.2 = ((bf16[16,64,256]{2,1,0:T(8,128)(2,1)}), bf16[16,64,256]{2,1,0:T(8,128)(2,1)S(1)}, u32[]{:S(2)}, u32[]{:S(2)}) async-start(bf16[16,64,256]{2,1,0:T(8,128)(2,1)} %select_select_fusion), calls=%async_computation.2 | async-start | bytes 1048576 | tf_op jit(solution)/shard_map/all_to_all | solution.py:101
  187.4 11.0 %copy-start.1 = (bf16[1152,256]{1,0:T(8,128)(2,1)S(1)}, bf16[1152,256]{1,0:T(8,128)(2,1)}, u32[]{:S(2)}) copy-start(bf16[1152,256]{1,0:T(8,128)(2,1)} %param.9) | copy-start | bytes 1769476
where the time goes:
time: 199 us; the launch traced here: 198 us
  blocking collectives  85.8 us (43%)
  matrix products  35.5 us (18%)
  starting transfers between devices  28.5 us (14%)
  other arithmetic  16.9 us (8%)
  local copies, waits for them, and re-layouts  16.4 us (8%)
  waiting for transfers between devices  15 us (8%)
    all_to_all x3, blocking collectives, copy_for_each(): lax.all_to_all(jnp.broadcast_to(value[None], (length, *value.shape)), axi...  56.7 us
    dot_general x8, matrix products, shards(): jnp.einsum('bij,bje->bie', selector, windows, preferred_element_type=jnp....  26.6 us
    all_to_all x1, blocking collectives, sum_in_two_steps(): return jnp.sum(lax.all_to_all(own, far, 0, 0, tiled=True), axis=0)  24.6 us
    all_to_all x1, waiting for transfers between devices, fetch_rows(): lax.all_to_all(fetched, PIX, split_axis=0, concat_axis=0, tiled=True)  15 us
    all_to_all x1, starting transfers between devices, fetch_rows(): lax.all_to_all(outgoing, PIX, split_axis=0, concat_axis=0, tiled=True)  9.9 us
    convert_element_type x1, other arithmetic, shards(): pixel_grad = summed.astype(jnp.bfloat16)  9.63 us
    all_to_all x1, starting transfers between devices, fetch_rows(): lax.all_to_all(fetched, PIX, split_axis=0, concat_axis=0, tiled=True)  7.48 us
    dot_general x1, matrix products, shards(): jnp.dot(spectra, enc_weight, preferred_element_type=jnp.float32)  4.99 us
  transfers between devices with their start and end apart: 5, of which 1 were waited for; matrix products, arithmetic and copies ran while one was open for 29% of the time, Pallas kernels for 0%

commit v1 on v0

--- a/solution.py
+++ b/solution.py
@@ -1,6 +1,8 @@
 import jax
 import jax.numpy as jnp
 from jax import lax
+from jax.experimental import pallas as pl
+from jax.experimental.pallas import tpu as pltpu
 from jax.sharding import Mesh
 from jax.sharding import PartitionSpec as P
 
@@ -8,6 +10,8 @@
 HALO = 128
 PIX = ("pix_0", "pix_1")
 OBS_PIX = ("obs", "pix_0", "pix_1")
+BF16 = jnp.bfloat16
+F32 = jnp.float32
 
 
 def extended(value, sides, width):
@@ -34,56 +38,6 @@
     return arrived.astype(jnp.float32).sum(axis=0)
 
 
-def laid_out(pieces, dim):
-    pieces = jnp.moveaxis(pieces, 0, dim)
-    dims = pieces.shape
-    return pieces.reshape(*dims[:dim], dims[dim] * dims[dim + 1], *dims[dim + 2 :])
-
-
-def copy_for_each(value, axis):
-    length = lax.axis_size(axis)
-    return lax.all_to_all(
-        jnp.broadcast_to(value[None], (length, *value.shape)), axis, 0, 0, tiled=True
-    )
-
-
-def collect(value, axis, dim):
-    return laid_out(copy_for_each(value, axis), dim)
-
-
-def rows_for(lines, length):
-    spare = -lines.shape[0] % length
-    if not spare:
-        return lines
-    return jnp.concatenate([lines, jnp.zeros((spare, *lines.shape[1:]), lines.dtype)])
-
-
-def gather_axes(value, axes, dim):
-    far, near = axes
-    first = copy_for_each(value, far)
-    pieces = jnp.swapaxes(copy_for_each(first, near), 0, 1)
-    return laid_out(pieces.reshape(-1, *value.shape), dim)
-
-
-def sum_at_owner(value, axis, dim):
-    pieces = in_blocks(value, dim, lax.axis_size(axis))
-    arrived = lax.all_to_all(pieces, axis, split_axis=0, concat_axis=0, tiled=True)
-    return arrived.sum(axis=0)
-
-
-def sum_in_two_steps(value, axes, dim):
-    far, near = axes
-    own = sum_at_owner(in_blocks(value, dim, lax.axis_size(far)), near, dim + 1)
-    return jnp.sum(lax.all_to_all(own, far, 0, 0, tiled=True), axis=0)
-
-
-def total_of(value, axes):
-    lines = value.reshape(-1, value.shape[-1])
-    padded = rows_for(lines, lax.axis_size(axes[0]) * lax.axis_size(axes[1]))
-    whole = gather_axes(sum_in_two_steps(padded, axes, 0), axes, 0)
-    return lax.slice_in_dim(whole, 0, len(lines)).reshape(value.shape)
-
-
 def fetch_rows(pixel_grad, tile_ids, local_ids, capacity):
     tile_count = lax.axis_size(PIX)
     feature_count = pixel_grad.shape[1]
@@ -106,6 +60,224 @@
     sigma = jax.nn.sigmoid(pre)
     deriv = sigma * (1.0 + pre * (1.0 - sigma))
     return (weights[:, None] * deriv * fetched.astype(jnp.float32)).astype(jnp.bfloat16)
+
+
+def send(source, target, send_sem, recv_sem, where):
+    return pltpu.make_async_remote_copy(
+        src_ref=source,
+        dst_ref=target,
+        send_sem=send_sem,
+        recv_sem=recv_sem,
+        device_id=where,
+        device_id_type=pl.DeviceIdType.MESH,
+    )
+
+
+def greet(groups):
+    barrier = pltpu.get_barrier_semaphore()
+    count = 0
+    for name, size in groups:
+        me = lax.axis_index(name)
+        for step in range(1, size):
+            pl.semaphore_signal(
+                barrier,
+                inc=1,
+                device_id={name: lax.rem(me + step, size)},
+                device_id_type=pl.DeviceIdType.MESH,
+            )
+            count += 1
+    pl.semaphore_wait(barrier, count)
+
+
+def gather_multiply(part, spec, spec_copies, shards, total, gs, gr):
+    y = lax.axis_index("chan")
+    right, left, far = lax.rem(y + 1, 4), lax.rem(y + 3, 4), lax.rem(y + 2, 4)
+    rows = part.shape[0]
+    lo, hi = pl.ds(0, rows // 2), pl.ds(rows // 2, rows // 2)
+    to_right, to_left = {"chan": right}, {"chan": left}
+    sends = [
+        send(part.at[lo], shards.at[y, lo], gs.at[0], gr.at[0], to_right),
+        send(part.at[hi], shards.at[y, hi], gs.at[1], gr.at[1], to_left),
+        send(part.at[hi], shards.at[y, hi], gs.at[2], gr.at[2], to_right),
+        send(part.at[lo], shards.at[y, lo], gs.at[3], gr.at[3], to_left),
+    ]
+    for copy in sends:
+        copy.start()
+
+    width = total.shape[1] // 3
+
+    def multiply(gradient, owner, step):
+        spec_copies[step].wait()
+        turned = jnp.transpose(gradient.astype(F32)).astype(BF16)
+        for n in range(3):
+            columns = pl.ds(n * width, width)
+            block = spec[pl.ds(pl.multiple_of(owner * rows, rows), rows), columns]
+            product = jnp.dot(turned, block, preferred_element_type=F32)
+            if step:
+                total[:, columns] += product
+            else:
+                total[:, columns] = product
+
+    multiply(part[...], y, 0)
+    send(part.at[lo], shards.at[left, lo], gs.at[0], gr.at[0], to_right).wait_recv()
+    sends.append(send(shards.at[left, lo], shards.at[left, lo], gs.at[4], gr.at[4], to_right))
+    sends[4].start()
+    send(part.at[hi], shards.at[right, hi], gs.at[1], gr.at[1], to_left).wait_recv()
+    sends.append(send(shards.at[right, hi], shards.at[right, hi], gs.at[5], gr.at[5], to_left))
+    sends[5].start()
+    send(part.at[hi], shards.at[left, hi], gs.at[2], gr.at[2], to_right).wait_recv()
+    multiply(shards[left], left, 1)
+    send(part.at[lo], shards.at[right, lo], gs.at[3], gr.at[3], to_left).wait_recv()
+    multiply(shards[right], right, 2)
+    send(part.at[lo], shards.at[far, lo], gs.at[4], gr.at[4], to_right).wait_recv()
+    send(part.at[hi], shards.at[far, hi], gs.at[5], gr.at[5], to_left).wait_recv()
+    multiply(shards[far], far, 3)
+    return sends
+
+
+def add_up(total, out, half_out, half_in, turned, xs, xr, zf, zs, zr, pieces, sems):
+    core_s, core_r, xs_s, xs_r, zs_s, zs_r, pz_s, pz_r, px_s, px_r, pc_s, pc_r = sems
+    x, z, c = (lax.axis_index(name) for name in ("obs", "pix_0", "pix_1"))
+    o = 1 - c
+    lines, wide = xs.shape[1], zf.shape[1]
+    sends = []
+
+    half_out[...] = total[pl.ds(pl.multiple_of(o * 128, 128), 128), :].astype(BF16)
+    swap = send(half_out, half_in, core_s, core_r, {"pix_1": o})
+    swap.start()
+    sends.append(swap)
+    swap.wait_recv()
+    mine = pl.ds(pl.multiple_of(c * 128, 128), 128)
+    for j in range(total.shape[1] // 128):
+        block = pl.ds(j * 128, 128)
+        turned[block, :] = jnp.transpose(total[mine, block] + half_in[:, block].astype(F32))
+
+    for j in range(4):
+        xs[j] = turned[pl.ds(j * lines, lines), :].astype(BF16)
+    for d in (1, 3, 2):
+        peer = lax.rem(x + d, 4)
+        copy = send(xs.at[peer], xr.at[x], xs_s.at[d - 1], xs_r.at[d - 1], {"obs": peer})
+        copy.start()
+        sends.append(copy)
+    summed = turned[pl.ds(pl.multiple_of(x * lines, 8), lines), :]
+    for d in (1, 3, 2):
+        origin = lax.rem(x + 4 - d, 4)
+        send(xs.at[0], xr.at[origin], xs_s.at[d - 1], xs_r.at[d - 1], {"obs": origin}).wait_recv()
+        summed = summed + xr[origin].astype(F32)
+    turned[pl.ds(0, lines), :] = summed
+
+    for j in range(8):
+        zf[j] = turned[pl.ds(j * wide, wide), :]
+        zs[j] = zf[j].astype(BF16)
+    steps = (1, 7, 2, 6, 3, 5, 4)
+    for d in steps:
+        peer = lax.rem(z + d, 8)
+        copy = send(zs.at[peer], zr.at[z], zs_s.at[d - 1], zs_r.at[d - 1], {"pix_0": peer})
+        copy.start()
+        sends.append(copy)
+    own = zf[z]
+    for d in steps:
+        origin = lax.rem(z + 8 - d, 8)
+        send(zs.at[0], zr.at[origin], zs_s.at[d - 1], zs_r.at[d - 1], {"pix_0": origin}).wait_recv()
+        own = own + zr[origin].astype(F32)
+    pieces[c, x, z] = own.astype(BF16)
+
+    for d in steps:
+        piece = pieces.at[c, x, z]
+        peer = lax.rem(z + d, 8)
+        copy = send(piece, piece, pz_s.at[d - 1], pz_r.at[d - 1], {"pix_0": peer})
+        copy.start()
+        sends.append(copy)
+    for d in (0,) + steps:
+        origin = lax.rem(z + 8 - d, 8)
+        piece = pieces.at[c, x, origin]
+        if d:
+            send(piece, piece, pz_s.at[d - 1], pz_r.at[d - 1], {"pix_0": origin}).wait_recv()
+        for e in (1, 3, 2):
+            at = d * 3 + e - 1
+            copy = send(piece, piece, px_s.at[at], px_r.at[at], {"obs": lax.rem(x + e, 4)})
+            copy.start()
+            sends.append(copy)
+    for e in (0, 1, 3, 2):
+        column = lax.rem(x + 4 - e, 4)
+        if e:
+            for d in (0,) + steps:
+                at = d * 3 + e - 1
+                piece = pieces.at[c, column, lax.rem(z + 8 - d, 8)]
+                send(piece, piece, px_s.at[at], px_r.at[at], {"obs": column}).wait_recv()
+        group = pieces.at[c, column]
+        copy = send(group, group, pc_s.at[e], pc_r.at[e], {"pix_1": o})
+        copy.start()
+        sends.append(copy)
+    for e in range(4):
+        group = pieces.at[o, lax.rem(x + 4 - e, 4)]
+        send(group, group, pc_s.at[e], pc_r.at[e], {"pix_1": o}).wait_recv()
+    for cc in range(2):
+        for xx in range(4):
+            for zz in range(8):
+                row = xx * lines + zz * wide
+                out[pl.ds(row, wide), pl.ds(cc * 128, 128)] = pieces[cc, xx, zz].astype(F32)
+    return sends
+
+
+def finish_kernel(spec_hbm, part, out, spec, shards, total, half_out, half_in, turned, xs, xr,
+                  zf, zs, zr, pieces, load_sems, gs, gr, *sems):
+    y = lax.axis_index("chan")
+    rows = part.shape[0]
+    spec_copies = []
+    for step, d in enumerate((0, 3, 1, 2)):
+        block = pl.ds(pl.multiple_of(lax.rem(y + d, 4) * rows, rows), rows)
+        copy = pltpu.make_async_copy(spec_hbm.at[block], spec.at[block], load_sems.at[step])
+        copy.start()
+        spec_copies.append(copy)
+    greet((("obs", 4), ("pix_0", 8), ("pix_1", 2), ("chan", 4)))
+    sends = gather_multiply(part, spec, spec_copies, shards, total, gs, gr)
+    sends += add_up(total, out, half_out, half_in, turned, xs, xr, zf, zs, zr, pieces, sems)
+    for copy in sends:
+        copy.wait_send()
+
+
+def finish(spectra, part):
+    rows, features = part.shape
+    channels = spectra.shape[1]
+    dma = pltpu.SemaphoreType.DMA
+    return pl.pallas_call(
+        finish_kernel,
+        out_shape=jax.ShapeDtypeStruct((channels, features), F32),
+        in_specs=[pl.BlockSpec(memory_space=pl.ANY), pl.BlockSpec(memory_space=pltpu.VMEM)],
+        out_specs=pl.BlockSpec(memory_space=pltpu.VMEM),
+        scratch_shapes=[
+            pltpu.VMEM(spectra.shape, BF16),
+            pltpu.VMEM((4, rows, features), BF16),
+            pltpu.VMEM((features, channels), F32),
+            pltpu.VMEM((features // 2, channels), BF16),
+            pltpu.VMEM((features // 2, channels), BF16),
+            pltpu.VMEM((channels, features // 2), F32),
+            pltpu.VMEM((4, channels // 4, features // 2), BF16),
+            pltpu.VMEM((4, channels // 4, features // 2), BF16),
+            pltpu.VMEM((8, channels // 32, features // 2), F32),
+            pltpu.VMEM((8, channels // 32, features // 2), BF16),
+            pltpu.VMEM((8, channels // 32, features // 2), BF16),
+            pltpu.VMEM((2, 4, 8, channels // 32, features // 2), BF16),
+            dma((4,)),
+            dma((6,)),
+            dma((6,)),
+            dma(()),
+            dma(()),
+            dma((3,)),
+            dma((3,)),
+            dma((7,)),
+            dma((7,)),
+            dma((7,)),
+            dma((7,)),
+            dma((24,)),
+            dma((24,)),
+            dma((4,)),
+            dma((4,)),
+        ],
+        compiler_params=pltpu.CompilerParams(collective_id=0, has_side_effects=True),
+        name="finish",
+    )(spectra, part)
 
 
 def shards(spectra, enc_weight, pix_tile, pix_local, foot_weight, cotangent, adjoint, mixing):
@@ -143,13 +315,7 @@
     weights = lax.dynamic_slice_in_dim(foot_weight, first_row, quarter, 0)
     fetched = fetch_rows(pixel_grad, tile_ids, local_ids, capacity_part)
     grad_part = pre_gradient(pre, fetched, weights)
-    local_grad = lax.dot_general(
-        spectra,
-        collect(grad_part, "chan", 0),
-        (((0,), (0,)), ((), ())),
-        preferred_element_type=jnp.float32,
-    )
-    return total_of(local_grad, (("obs", "pix_0"), "pix_1"))
+    return finish(spectra, grad_part)
 
 
 def solution(mesh):

time: 199 us -> 150 us (0.75)
  blocking collectives: 85.8 us -> 0 us
  Pallas kernels: 0 us -> 42.1 us
  matrix products: 35.5 us -> 31.6 us
    all_to_all x5 -> x0, blocking collectives: 85.8 us -> none  [the longest x3 56.7 us: copy_for_each(): lax.all_to_all(jnp.broadcast_to(value[None], (length, *value.shape)), axi...]
    pallas_call x0 -> x1, Pallas kernels: none -> 42.1 us  [finish(): pl.pallas_call(finish_kernel, out_shape=jax.ShapeDtypeStruct((channels, f...]
    dot_general x1 -> x0, matrix products: 3.89 us -> none  [shards(): lax.dot_general(spectra, collect(grad_part, 'chan', 0), (((0,), (0,)), ((...]
    unnamed x10 -> x9, local copies, waits for them, and re-layouts: 0.03 us -> 2.38 us
  transfers between devices with their start and end apart: 5 -> 5, of which waited for: 1 -> 1; matrix products, arithmetic and copies ran while one was open for 29% -> 38% of each run, Pallas kernels for 0% -> 0%
where the time goes in v1:
time: 150 us
  Pallas kernels  42.1 us (28%)
  matrix products  31.6 us (21%)
  starting transfers between devices  28.5 us (19%)
  other arithmetic  17.4 us (12%)
  waiting for transfers between devices  15 us (10%)
  local copies, waits for them, and re-layouts  14.8 us (10%)
    pallas_call x1, Pallas kernels, finish(): pl.pallas_call(finish_kernel, out_shape=jax.ShapeDtypeStruct((channels, f...  42.1 us
    dot_general x8, matrix products, shards(): jnp.einsum('bij,bje->bie', selector, windows, preferred_element_type=jnp....  26.6 us
    all_to_all x1, waiting for transfers between devices, fetch_rows(): lax.all_to_all(fetched, PIX, split_axis=0, concat_axis=0, tiled=True)  15 us
    all_to_all x1, starting transfers between devices, fetch_rows(): lax.all_to_all(outgoing, PIX, split_axis=0, concat_axis=0, tiled=True)  9.9 us
    convert_element_type x1, other arithmetic, shards(): pixel_grad = summed.astype(jnp.bfloat16)  9.61 us
    all_to_all x1, starting transfers between devices, fetch_rows(): lax.all_to_all(fetched, PIX, split_axis=0, concat_axis=0, tiled=True)  7.48 us
    dot_general x1, matrix products, shards(): jnp.dot(spectra, enc_weight, preferred_element_type=jnp.float32)  4.99 us
    ppermute x1, starting transfers between devices, extended(): before = lax.ppermute(last, axis, up)  4.92 us
  transfers between devices with their start and end apart: 5, of which 1 were waited for; matrix products, arithmetic and copies ran while one was open for 38% of the time, Pallas kernels for 0%

profile of v1, /device:TPU:1, one launch (start us, length us, event | category | flops | bytes accessed | tf_op | source)
XLA Modules:
  0.0 149.7 jit_solution(1082345363747329600)
XLA Ops:
  0.9 4.9 %collective-permute-start = (bf16[128,256]{1,0:T(8,128)(2,1)S(1)}, bf16[128,256]{1,0:T(8,128)(2,1)S(1)}, u32[]{:S(2)}, u32[]{:S(2)}) collective-permute-start(bf16[128,256]{1,0:T(8,128)(2,1)S(1)} %get-tuple-element.9), channel_id=1, source_target_pairs={{0,4},{4,8},{8,12},{12,16},{16,20},{20,24},{24,28},{28,32},{32,36}... | collective-permute-start | bytes 196616 | tf_op jit(solution)/shard_map/ppermute | solution.py:24
  5.9 1.9 %collective-permute-start.1 = (bf16[128,256]{1,0:T(8,128)(2,1)S(1)}, bf16[128,256]{1,0:T(8,128)(2,1)S(1)}, u32[]{:S(2)}, u32[]{:S(2)}) collective-permute-start(bf16[128,256]{1,0:T(8,128)(2,1)S(1)} %get-tuple-element.10), channel_id=1, source_target_pairs={{4,0},{8,4},{12,8},{16,12},{20,16},{24,20},{28,24},{32,28},{36,32}... | collective-permute-start | bytes 196616 | tf_op jit(solution)/shard_map/ppermute | solution.py:25
  8.5 1.1 reduce-window.6
  11.5 2.4 %scatter_custom_fusion = s32[1024]{0:T(1024)S(1)} fusion(s32[512]{0:T(512)S(1)} %bitcast.134, s32[512]{0:T(512)S(1)} %dynamic_slice.11, s32[]{:T(128)} %constant.37.clone.1), kind=kCustom, calls=%fused_computation.84 | custom fusion | bytes 4100 | tf_op jit(solution)/shard_map/scatter | solution.py:49
  14.6 9.9 %all-to-all-start.1 = ((s32[16,1,64]{2,1,0:T(1,128)}), s32[16,1,64]{2,1,0:T(1,128)S(1)}, u32[]{:S(2)}, u32[]{:S(2)}) async-start(s32[16,1,64]{2,1,0:T(1,128)} %all_to_all.17), calls=%async_computation.1 | async-start | bytes 16384 | tf_op jit(solution)/shard_map/all_to_all | solution.py:51
  24.5 1.9 %slice_subtract_fusion.7 = (s32[1,4096]{1,0:T(1,128)S(1)}, s32[1,4096]{1,0:T(1,128)S(1)}, s32[1,4096]{1,0:T(1,128)S(1)}, s32[1,4096]{1,0:T(1,128)S(1)}, s32[1,40...) fusion(s32[8,4096]{1,0:T(8,128)} %param.14, s32[]{:T(128)S(6)} %sub.212), kind=kLoop, calls=%fused_computation.69 | loop fusion | flops 32768 | bytes 262148 | tf_op jit(solution)/shard_map/sub | solution.py:299
  26.5 5.0 %convolution_convert_fusion = bf16[2048,256]{1,0:T(8,128)(2,1)} fusion(bf16[2048,1152]{1,0:T(8,128)(2,1)} %spec_hbm.1, bf16[1152,256]{1,0:T(8,128)(2,1)S(1)} %copy-done), kind=kOutput, calls=%fused_computation.45 | convolution fusion | flops 1208483840 | bytes 6356992 | tf_op jit(solution)/shard_map/dot_general | solution.py:308
  31.6 4.3 %all-to-all-start = ((bf16[4,512,256]{2,1,0:T(8,128)(2,1)}), bf16[4,512,256]{2,1,0:T(8,128)(2,1)}, u32[]{:S(2)}, u32[]{:S(2)}) async-start(bf16[4,512,256]{2,1,0:T(8,128)(2,1)} %bitcast.121), calls=%async_computation | async-start | bytes 2097152 | tf_op jit(solution)/shard_map/all_to_all | solution.py:37
  36.3 2.9 %fusion = f32[32,128,256]{2,1,0:T(8,128)S(1)} fusion(s32[32,128]{1,0:T(8,128)S(1)} %get-tuple-element.29, bf16[32,128,256]{2,1,0:T(8,128)(2,1)S(1)} %bitcast.112, bf16[32,128,256]{2,1,0:T(8,128)(2,1)S(1)} %bitcast.96, bf16[32,128,256]{2,1,0:T(8,128)(2,1)S(1)} %bitcast.104), kind=kOutput, calls=%fused_computation.12 | convolution fusion | flops 825753600 | bytes 10502144 | tf_op jit(solution)/shard_map/bij,bje->bie/dot_general | solution.py:301
  39.2 2.9 %fusion.1 = f32[32,128,256]{2,1,0:T(8,128)S(1)} fusion(s32[32,128]{1,0:T(8,128)S(1)} %get-tuple-element.30, bf16[32,128,256]{2,1,0:T(8,128)(2,1)S(1)} %bitcast.113, bf16[32,128,256]{2,1,0:T(8,128)(2,1)S(1)} %bitcast.97, bf16[32,128,256]{2,1,0:T(8,128)(2,1)S(1)} %bitcast.105), kind=kOutput, calls=%fused_computation.13 | convolution fusion | flops 825753600 | bytes 10502144 | tf_op jit(solution)/shard_map/bij,bje->bie/dot_general | solution.py:301
  42.0 3.5 %fusion.2 = f32[32,128,256]{2,1,0:T(8,128)} fusion(s32[32,128]{1,0:T(8,128)S(1)} %get-tuple-element.31, bf16[32,128,256]{2,1,0:T(8,128)(2,1)S(1)} %bitcast.114, bf16[32,128,256]{2,1,0:T(8,128)(2,1)S(1)} %bitcast.98, bf16[32,128,256]{2,1,0:T(8,128)(2,1)S(1)} %bitcast.106), kind=kOutput, calls=%fused_computation.14 | convolution fusion | flops 825753600 | bytes 10502144 | tf_op jit(solution)/shard_map/bij,bje->bie/dot_general | solution.py:301
  45.5 3.5 %fusion.3 = f32[32,128,256]{2,1,0:T(8,128)} fusion(s32[32,128]{1,0:T(8,128)S(1)} %get-tuple-element.32, bf16[32,128,256]{2,1,0:T(8,128)(2,1)S(1)} %bitcast.115, bf16[32,128,256]{2,1,0:T(8,128)(2,1)S(1)} %bitcast.99, bf16[32,128,256]{2,1,0:T(8,128)(2,1)S(1)} %bitcast.107), kind=kOutput, calls=%fused_computation.15 | convolution fusion | flops 825753600 | bytes 10502144 | tf_op jit(solution)/shard_map/bij,bje->bie/dot_general | solution.py:301
  49.0 3.5 %fusion.4 = f32[32,128,256]{2,1,0:T(8,128)} fusion(s32[32,128]{1,0:T(8,128)S(1)} %get-tuple-element.33, bf16[32,128,256]{2,1,0:T(8,128)(2,1)S(1)} %bitcast.116, bf16[32,128,256]{2,1,0:T(8,128)(2,1)S(1)} %bitcast.100, bf16[32,128,256]{2,1,0:T(8,128)(2,1)S(1)} %bitcast.108), kind=kOutput, calls=%fused_computation.16 | convolution fusion | flops 825753600 | bytes 10502144 | tf_op jit(solution)/shard_map/bij,bje->bie/dot_general | solution.py:301
  52.5 3.5 %fusion.5 = f32[32,128,256]{2,1,0:T(8,128)} fusion(s32[32,128]{1,0:T(8,128)S(1)} %get-tuple-element.34, bf16[32,128,256]{2,1,0:T(8,128)(2,1)S(1)} %bitcast.117, bf16[32,128,256]{2,1,0:T(8,128)(2,1)S(1)} %bitcast.101, bf16[32,128,256]{2,1,0:T(8,128)(2,1)S(1)} %bitcast.109), kind=kOutput, calls=%fused_computation.17 | convolution fusion | flops 825753600 | bytes 10502144 | tf_op jit(solution)/shard_map/bij,bje->bie/dot_general | solution.py:301
  56.0 3.5 %fusion.6 = f32[32,128,256]{2,1,0:T(8,128)} fusion(s32[32,128]{1,0:T(8,128)S(1)} %get-tuple-element.35, bf16[32,128,256]{2,1,0:T(8,128)(2,1)S(1)} %bitcast.118, bf16[32,128,256]{2,1,0:T(8,128)(2,1)S(1)} %bitcast.102, bf16[32,128,256]{2,1,0:T(8,128)(2,1)S(1)} %bitcast.110), kind=kOutput, calls=%fused_computation.18 | convolution fusion | flops 825753600 | bytes 10502144 | tf_op jit(solution)/shard_map/bij,bje->bie/dot_general | solution.py:301
  59.5 3.5 %fusion.7 = f32[32,128,256]{2,1,0:T(8,128)} fusion(s32[32,128]{1,0:T(8,128)S(1)} %get-tuple-element.36, bf16[32,128,256]{2,1,0:T(8,128)(2,1)S(1)} %bitcast.119, bf16[32,128,256]{2,1,0:T(8,128)(2,1)S(1)} %bitcast.103, bf16[32,128,256]{2,1,0:T(8,128)(2,1)S(1)} %bitcast.111), kind=kOutput, calls=%fused_computation.19 | convolution fusion | flops 825753600 | bytes 10502144 | tf_op jit(solution)/shard_map/bij,bje->bie/dot_general | solution.py:301
  62.9 9.6 %fusion.9 = bf16[4096,256]{1,0:T(8,128)(2,1)S(1)} fusion(f32[32,128,256]{2,1,0:T(8,128)} %fusion.7, f32[32,128,256]{2,1,0:T(8,128)} %fusion.6, f32[32,128,256]{2,1,0:T(8,128)} %fusion.5, f32[32,128,256]{2,1,0:T(8,128)} %fusion.4, f32[32,128,256]{2,1,0:T(8,128)} %fusion.3, f32[32,128,256]{2,1,0:T(8,128)} %fusion.2, f32[32,128,256]{2,1,0:T(8,128)S(1)} %fusion.1, ...), kind=kLoop, calls=%fused_computation.22 | loop fusion | flops 18874368 | bytes 37756928 | tf_op jit(solution)/shard_map/convert_element_type | solution.py:303
  72.6 3.9 %gather_fusion = bf16[1024,256]{1,0:T(8,128)(2,1)S(1)} fusion(bf16[4096,256]{1,0:T(8,128)(2,1)S(1)} %fusion.9, s32[1024]{0:T(1024)S(1)} %broadcast_clamp_fusion), kind=kCustom, calls=%fused_computation | custom fusion | bytes 1052672 | tf_op jit(solution)/shard_map/jit(_take)/gather | solution.py:53
  77.6 7.5 %all-to-all-start.2 = ((bf16[16,64,256]{2,1,0:T(8,128)(2,1)}), bf16[16,64,256]{2,1,0:T(8,128)(2,1)S(1)}, u32[]{:S(2)}, u32[]{:S(2)}) async-start(bf16[16,64,256]{2,1,0:T(8,128)(2,1)} %select_select_fusion), calls=%async_computation.2 | async-start | bytes 1048576 | tf_op jit(solution)/shard_map/all_to_all | solution.py:55
  85.9 1.4 convert_reduce_fusion
  87.3 15.0 %all-to-all-done.2 = bf16[16,64,256]{2,1,0:T(8,128)(2,1)S(1)} async-done(((bf16[16,64,256]{2,1,0:T(8,128)(2,1)}), bf16[16,64,256]{2,1,0:T(8,128)(2,1)S(1)}, u32[]{:S(2)}, u32[]{:S(2)}) %all-to-all-start.2) | async-done | bytes 524320 | tf_op jit(solution)/shard_map/all_to_all | solution.py:55
  102.3 1.9 %gather_fusion.1 = bf16[512,256]{1,0:T(8,128)(2,1)S(1)} fusion(bf16[1024,256]{1,0:T(8,128)(2,1)S(1)} %bitcast.95, s32[1024]{0:T(1024)S(1)} %pad_clamp_fusion), kind=kCustom, calls=%fused_computation.1 | custom fusion | bytes 526336 | tf_op jit(solution)/shard_map/jit(_take)/gather | solution.py:56
  105.3 42.1 %finish.1 = f32[1152,256]{1,0:T(8,128)} custom-call(bf16[2048,1152]{1,0:T(8,128)(2,1)} %spec_hbm.1, bf16[512,256]{1,0:T(8,128)(2,1)} %multiply_convert_fusion.part), custom_call_target="tpu_custom_call" | custom-call | tf_op jit(solution)/shard_map/finish/pallas_call | solution.py:244
  147.4 2.4 %copy.14 = f32[1152,256]{1,0:T(8,128)} copy(f32[1152,256]{1,0:T(8,128)} %finish.1) | data formatting | bytes 2359296
  (34 shorter events, 7.5 us)
Async XLA Ops:
  0.0 26.5 %copy-start = (bf16[1152,256]{1,0:T(8,128)(2,1)S(1)}, bf16[1152,256]{1,0:T(8,128)(2,1)}, u32[]{:S(2)}) copy-start(bf16[1152,256]{1,0:T(8,128)(2,1)} %param.9) | copy-start | bytes 1769476
  0.9 35.0 %collective-permute-start = (bf16[128,256]{1,0:T(8,128)(2,1)S(1)}, bf16[128,256]{1,0:T(8,128)(2,1)S(1)}, u32[]{:S(2)}, u32[]{:S(2)}) collective-permute-start(bf16[128,256]{1,0:T(8,128)(2,1)S(1)} %get-tuple-element.9), channel_id=1, source_target_pairs={{0,4},{4,8},{8,12},{12,16},{16,20},{20,24},{24,28},{28,32},{32,36}... | collective-permute-start | bytes 196616 | tf_op jit(solution)/shard_map/ppermute | solution.py:24
  5.9 30.1 %collective-permute-start.1 = (bf16[128,256]{1,0:T(8,128)(2,1)S(1)}, bf16[128,256]{1,0:T(8,128)(2,1)S(1)}, u32[]{:S(2)}, u32[]{:S(2)}) collective-permute-start(bf16[128,256]{1,0:T(8,128)(2,1)S(1)} %get-tuple-element.10), channel_id=1, source_target_pairs={{4,0},{8,4},{12,8},{16,12},{20,16},{24,20},{28,24},{32,28},{36,32}... | collective-permute-start | bytes 196616 | tf_op jit(solution)/shard_map/ppermute | solution.py:25
  14.6 17.0 %all-to-all-start.1 = ((s32[16,1,64]{2,1,0:T(1,128)}), s32[16,1,64]{2,1,0:T(1,128)S(1)}, u32[]{:S(2)}, u32[]{:S(2)}) async-start(s32[16,1,64]{2,1,0:T(1,128)} %all_to_all.17), calls=%async_computation.1 | async-start | bytes 16384 | tf_op jit(solution)/shard_map/all_to_all | solution.py:51
  26.5 5.1 %copy-start.3 = (f32[8,256]{1,0:T(8,128)S(1)}, f32[8,256]{1,0:T(8,128)}, u32[]{:S(2)}) copy-start(f32[8,256]{1,0:T(8,128)} %param.15) | copy-start | bytes 24580
  26.5 9.5 %copy-start.1 = (bf16[4096,256]{1,0:T(8,128)(2,1)S(1)}, bf16[4096,256]{1,0:T(8,128)(2,1)}, u32[]{:S(2)}) copy-start(bf16[4096,256]{1,0:T(8,128)(2,1)} %param.13) | copy-start | bytes 6291460
  31.6 46.0 %all-to-all-start = ((bf16[4,512,256]{2,1,0:T(8,128)(2,1)}), bf16[4,512,256]{2,1,0:T(8,128)(2,1)}, u32[]{:S(2)}, u32[]{:S(2)}) async-start(bf16[4,512,256]{2,1,0:T(8,128)(2,1)} %bitcast.121), calls=%async_computation | async-start | bytes 2097152 | tf_op jit(solution)/shard_map/all_to_all | solution.py:37
  59.5 3.5 %copy-start.2 = (bf16[4096,256]{1,0:T(8,128)(2,1)S(1)}, bf16[4096,256]{1,0:T(8,128)(2,1)}, u32[]{:S(2)}) copy-start(bf16[4096,256]{1,0:T(8,128)(2,1)} %param.13) | copy-start | bytes 6291460
  77.6 24.7 %all-to-all-start.2 = ((bf16[16,64,256]{2,1,0:T(8,128)(2,1)}), bf16[16,64,256]{2,1,0:T(8,128)(2,1)S(1)}, u32[]{:S(2)}, u32[]{:S(2)}) async-start(bf16[16,64,256]{2,1,0:T(8,128)(2,1)} %select_select_fusion), calls=%async_computation.2 | async-start | bytes 1048576 | tf_op jit(solution)/shard_map/all_to_all | solution.py:55

commit v2 on v1

v2 whole, which is shorter than its diff:
```python
import jax
import jax.numpy as jnp
from jax import lax
from jax.experimental import pallas as pl
from jax.experimental.pallas import tpu as pltpu
from jax.sharding import Mesh
from jax.sharding import PartitionSpec as P

TILE = 4096
CAP = 64
STEPS = (4, 3, 5, 2, 6, 1, 7, 0)
PIX = ("pix_0", "pix_1")
OBS_PIX = ("obs", "pix_0", "pix_1")
AXES = ("obs", "pix_0", "pix_1", "chan")
BF16 = jnp.bfloat16
F32 = jnp.float32


def send(source, target, send_sem, recv_sem, where):
    return pltpu.make_async_remote_copy(
        src_ref=source,
        dst_ref=target,
        send_sem=send_sem,
        recv_sem=recv_sem,
        device_id=where,
        device_id_type=pl.DeviceIdType.MESH,
    )


def greet():
    barrier = pltpu.get_barrier_semaphore()
    x, z, c, y = (lax.axis_index(name) for name in AXES)
    peers = [{"obs": lax.rem(x + d, 4)} for d in range(1, 4)]
    peers += [{"chan": lax.rem(y + d, 4)} for d in range(1, 4)]
    for d in range(8):
        for e in range(2):
            if d or e:
                peers.append({"pix_0": lax.rem(z + d, 8), "pix_1": lax.rem(c + e, 2)})
    for peer in peers:
        pl.semaphore_signal(
            barrier, inc=1, device_id=peer, device_id_type=pl.DeviceIdType.MESH
        )
    return barrier, len(peers)


def gather_multiply(part, spec, shards, total, gs, gr):
    y = lax.axis_index("chan")
    right, left, far = lax.rem(y + 1, 4), lax.rem(y + 3, 4), lax.rem(y + 2, 4)
    rows = part.shape[0]
    lo, hi = pl.ds(0, rows // 2), pl.ds(rows // 2, rows // 2)
    to_right, to_left = {"chan": right}, {"chan": left}
    sends = [
        send(part.at[lo], shards.at[y, lo], gs.at[0], gr.at[0], to_right),
        send(part.at[hi], shards.at[y, hi], gs.at[1], gr.at[1], to_left),
        send(part.at[hi], shards.at[y, hi], gs.at[2], gr.at[2], to_right),
        send(part.at[lo], shards.at[y, lo], gs.at[3], gr.at[3], to_left),
    ]
    for copy in sends:
        copy.start()

    width = total.shape[1] // 3

    def multiply(gradient, owner, step):
        turned = jnp.transpose(gradient.astype(F32)).astype(BF16)
        for n in range(3):
            columns = pl.ds(n * width, width)
            block = spec[pl.ds(pl.multiple_of(owner * rows, rows), rows), columns]
            product = jnp.dot(turned, block, preferred_element_type=F32)
            if step:
                total[:, columns] += product
            else:
                total[:, columns] = product

    multiply(part[...], y, 0)
    send(part.at[lo], shards.at[left, lo], gs.at[0], gr.at[0], to_right).wait_recv()
    sends.append(send(shards.at[left, lo], shards.at[left, lo], gs.at[4], gr.at[4], to_right))
    sends[4].start()
    send(part.at[hi], shards.at[right, hi], gs.at[1], gr.at[1], to_left).wait_recv()
    sends.append(send(shards.at[right, hi], shards.at[right, hi], gs.at[5], gr.at[5], to_left))
    sends[5].start()
    send(part.at[hi], shards.at[left, hi], gs.at[2], gr.at[2], to_right).wait_recv()
    multiply(shards[left], left, 1)
    send(part.at[lo], shards.at[right, lo], gs.at[3], gr.at[3], to_left).wait_recv()
    multiply(shards[right], right, 2)
    send(part.at[lo], shards.at[far, lo], gs.at[4], gr.at[4], to_right).wait_recv()
    send(part.at[hi], shards.at[far, hi], gs.at[5], gr.at[5], to_left).wait_recv()
    multiply(shards[far], far, 3)
    return sends


def add_up(total, out, half_out, half_in, turned, xs, xr, zf, zs, zr, pieces, sems):
    core_s, core_r, xs_s, xs_r, zs_s, zs_r, pz_s, pz_r, px_s, px_r, pc_s, pc_r = sems
    x, z, c = (lax.axis_index(name) for name in ("obs", "pix_0", "pix_1"))
    o = 1 - c
    lines, wide = xs.shape[1], zf.shape[1]
    sends = []

    half_out[...] = total[pl.ds(pl.multiple_of(o * 128, 128), 128), :].astype(BF16)
    swap = send(half_out, half_in, core_s, core_r, {"pix_1": o})
    swap.start()
    sends.append(swap)
    swap.wait_recv()
    mine = pl.ds(pl.multiple_of(c * 128, 128), 128)
    for j in range(total.shape[1] // 128):
        block = pl.ds(j * 128, 128)
        turned[block, :] = jnp.transpose(total[mine, block] + half_in[:, block].astype(F32))

    for j in range(4):
        xs[j] = turned[pl.ds(j * lines, lines), :].astype(BF16)
    for d in (1, 3, 2):
        peer = lax.rem(x + d, 4)
        copy = send(xs.at[peer], xr.at[x], xs_s.at[d - 1], xs_r.at[d - 1], {"obs": peer})
        copy.start()
        sends.append(copy)
    summed = turned[pl.ds(pl.multiple_of(x * lines, 8), lines), :]
    for d in (1, 3, 2):
        origin = lax.rem(x + 4 - d, 4)
        send(xs.at[0], xr.at[origin], xs_s.at[d - 1], xs_r.at[d - 1], {"obs": origin}).wait_recv()
        summed = summed + xr[origin].astype(F32)
    turned[pl.ds(0, lines), :] = summed

    for j in range(8):
        zf[j] = turned[pl.ds(j * wide, wide), :]
        zs[j] = zf[j].astype(BF16)
    steps = (1, 7, 2, 6, 3, 5, 4)
    for d in steps:
        peer = lax.rem(z + d, 8)
        copy = send(zs.at[peer], zr.at[z], zs_s.at[d - 1], zs_r.at[d - 1], {"pix_0": peer})
        copy.start()
        sends.append(copy)
    own = zf[z]
    for d in steps:
        origin = lax.rem(z + 8 - d, 8)
        send(zs.at[0], zr.at[origin], zs_s.at[d - 1], zs_r.at[d - 1], {"pix_0": origin}).wait_recv()
        own = own + zr[origin].astype(F32)
    pieces[c, x, z] = own.astype(BF16)

    for d in steps:
        piece = pieces.at[c, x, z]
        peer = lax.rem(z + d, 8)
        copy = send(piece, piece, pz_s.at[d - 1], pz_r.at[d - 1], {"pix_0": peer})
        copy.start()
        sends.append(copy)
    for d in (0,) + steps:
        origin = lax.rem(z + 8 - d, 8)
        piece = pieces.at[c, x, origin]
        if d:
            send(piece, piece, pz_s.at[d - 1], pz_r.at[d - 1], {"pix_0": origin}).wait_recv()
        for e in (1, 3, 2):
            at = d * 3 + e - 1
            copy = send(piece, piece, px_s.at[at], px_r.at[at], {"obs": lax.rem(x + e, 4)})
            copy.start()
            sends.append(copy)
    for e in (0, 1, 3, 2):
        column = lax.rem(x + 4 - e, 4)
        if e:
            for d in (0,) + steps:
                at = d * 3 + e - 1
                piece = pieces.at[c, column, lax.rem(z + 8 - d, 8)]
                send(piece, piece, px_s.at[at], px_r.at[at], {"obs": column}).wait_recv()
        group = pieces.at[c, column]
        copy = send(group, group, pc_s.at[e], pc_r.at[e], {"pix_1": o})
        copy.start()
        sends.append(copy)
    for e in range(4):
        group = pieces.at[o, lax.rem(x + 4 - e, 4)]
        send(group, group, pc_s.at[e], pc_r.at[e], {"pix_1": o}).wait_recv()
    for cc in range(2):
        for xx in range(4):
            for zz in range(8):
                row = xx * lines + zz * wide
                out[pl.ds(row, wide), pl.ds(cc * 128, 128)] = pieces[cc, xx, zz].astype(F32)
    return sends


def one_hot(condition):
    return jnp.where(condition, 1.0, 0.0).astype(BF16)


def iota(shape, dim):
    return lax.broadcasted_iota(jnp.int32, shape, dim)


def own_rows(ref, y):
    return jnp.concatenate([ref[pl.ds(4 * y + j, 1), :] for j in range(4)], axis=1)


def ask(tile, local, weight, y, asked, columns):
    tiles, locals_, weights = own_rows(tile, y), own_rows(local, y), own_rows(weight, y)
    rows = tiles.shape[1]
    named = jnp.broadcast_to(tiles, (16, rows)) == iota((16, rows), 0)
    earlier = one_hot(iota((rows, rows), 0) < iota((rows, rows), 1))
    counts = jnp.dot(one_hot(named), earlier, preferred_element_type=F32)
    rank = jnp.sum(jnp.where(named, counts, 0.0), axis=0, keepdims=True)
    placed = one_hot(jnp.broadcast_to(rank, (128, rows)) == iota((128, rows), 0).astype(F32))
    high = lax.shift_right_logical(locals_, 6)
    low = locals_ - high * 64
    wanted = jnp.zeros((16, 128), F32)
    for digit, scale in ((high, 64.0), (low, 1.0)):
        held = jnp.where(named, jnp.broadcast_to(digit.astype(F32), (16, rows)), 0.0).astype(BF16)
        wanted += scale * lax.dot_general(
            held, placed, (((1,), (1,)), ((), ())), preferred_element_type=F32
        )
    for t in range(16):
        asked[t] = wanted[t : t + 1, :]
    slot = tiles.astype(F32) * CAP + rank
    both = jnp.where(iota((128, rows), 0) == 0, jnp.broadcast_to(slot, (128, rows)),
                     jnp.broadcast_to(weights, (128, rows)))
    for j in range(rows // 128):
        block = pl.ds(j * 128, 128)
        columns[block, :] = jnp.transpose(both[:, j * 128 : (j + 1) * 128])


def spread(cot, adjoint, mixing, table, tile):
    block = 128
    lanes = iota((block, 3 * block), 1).astype(F32)

    def body(b, carry):
        start = pl.multiple_of(b * block, block)
        first = tile * TILE + start - block
        within = (adjoint[:, pl.ds(start, block)] - first).astype(F32)
        within = jnp.transpose(within)
        window = cot[pl.ds(start, 3 * block), :]
        total = window[block : 2 * block].astype(F32)
        for k in range(8):
            chosen = one_hot(jnp.broadcast_to(within[:, k : k + 1], lanes.shape) == lanes)
            picked = jnp.dot(chosen, window, preferred_element_type=F32)
            total = total + picked * mixing[pl.ds(k, 1), :]
        table[pl.ds(start, block), :] = total.astype(BF16)
        return carry

    lax.fori_loop(0, TILE // block, body, 0, unroll=2)


def answer(requests, table, start, answers):
    step = 512
    wanted = jnp.concatenate(
        [requests[0:CAP, k : k + 1] for k in range(start, start + 8)], axis=0
    )
    wanted = jnp.broadcast_to(wanted, (8 * CAP, step))
    lanes = iota((8 * CAP, step), 1).astype(F32)
    total = jnp.zeros((8 * CAP, table.shape[1]), F32)
    for j in range(TILE // step):
        chosen = one_hot(wanted - float(j * step) == lanes)
        total += jnp.dot(chosen, table[pl.ds(j * step, step), :], preferred_element_type=F32)
    for k in range(8):
        answers[start + k] = total[k * CAP : (k + 1) * CAP].astype(BF16)


def sums_of_parts(spec, spec_copies, weight, parts, parts_in, rs, rr, before_sends):
    y = lax.axis_index("chan")
    rows = parts.shape[1]
    sends = []
    for step, d in enumerate((2, 1, 3, 0)):
        peer = lax.rem(y + d, 4)
        spec_copies[step].wait()
        block = spec[pl.ds(pl.multiple_of(peer * rows, rows), rows), :]
        parts[peer] = jnp.dot(block, weight[...], preferred_element_type=F32).astype(BF16)
        if step == 0:
            before_sends()
        if d:
            copy = send(parts.at[peer], parts_in.at[y], rs.at[d - 1], rr.at[d - 1], {"chan": peer})
            copy.start()
            sends.append(copy)
    return sends


def whole_kernel(spec_hbm, weight, tile, local, foot, cot_hbm, adjoint, mixing, out, spec, cot,
                 table, parts, parts_in, asked, asked_in, square, columns, answers, answers_in,
                 part, shards, total, half_out, half_in, turned, xs, xr, zf, zs, zr, pieces,
                 result, load_sems, cot_sem, halo_s, halo_r, ask_s, ask_r, ans_s, ans_r, rs, rr,
                 gs, gr, *sems):
    x, z, c, y = (lax.axis_index(name) for name in AXES)
    me = z * 2 + c
    rows = part.shape[0]
    barrier, count = greet()
    spec_copies = []
    for step, d in enumerate((2, 1, 3, 0)):
        block = pl.ds(pl.multiple_of(lax.rem(y + d, 4) * rows, rows), rows)
        copy = pltpu.make_async_copy(spec_hbm.at[block], spec.at[block], load_sems.at[step])
        copy.start()
        spec_copies.append(copy)
    cot_copy = pltpu.make_async_copy(cot_hbm, cot.at[pl.ds(128, TILE)], cot_sem)
    cot_copy.start()
    ask(tile, local, foot, y, asked, columns)
    sends = []

    after = {"pix_0": lax.rem(z + c, 8), "pix_1": 1 - c}
    before = {"pix_0": lax.rem(z + 7 + c, 8), "pix_1": 1 - c}
    halos = [
        send(cot_hbm.at[pl.ds(0, 128)], cot.at[pl.ds(TILE + 128, 128)], halo_s.at[0],
             halo_r.at[0], before),
        send(cot_hbm.at[pl.ds(TILE - 128, 128)], cot.at[pl.ds(0, 128)], halo_s.at[1],
             halo_r.at[1], after),
    ]
    order = [(d, e) for d in STEPS for e in (1, 0)]

    def pair(k, ahead):
        d, e = order[k]
        other = lax.rem(c + e, 2)
        return lax.rem(z + (d if ahead else 8 - d), 8), other

    def first_sends():
        pl.semaphore_wait(barrier, count)
        for k in range(15):
            zz, cc = pair(k, True)
            copy = send(asked.at[zz * 2 + cc], asked_in.at[me], ask_s.at[k], ask_r.at[k],
                        {"pix_0": zz, "pix_1": cc})
            copy.start()
            sends.append(copy)
        for copy in halos:
            copy.start()
            sends.append(copy)

    sends += sums_of_parts(spec, spec_copies, weight, parts, parts_in, rs, rr, first_sends)
    cot_copy.wait()
    for copy in halos:
        copy.wait_recv()
    spread(cot, adjoint, mixing, table, me)

    square[...] = jnp.zeros_like(square)
    for k in range(15):
        zz, cc = pair(k, False)
        send(asked.at[0], asked_in.at[zz * 2 + cc], ask_s.at[k], ask_r.at[k],
             {"pix_0": zz, "pix_1": cc}).wait_recv()
        square[pl.ds(k, 1), :] = asked_in[zz * 2 + cc]
    square[pl.ds(15, 1), :] = asked[me]
    requests = jnp.transpose(square[...])
    for start in (0, 8):
        answer(requests, table, start, answers)
        for k in range(start, min(start + 8, 15)):
            zz, cc = pair(k, False)
            copy = send(answers.at[k], answers_in.at[me], ans_s.at[k], ans_r.at[k],
                        {"pix_0": zz, "pix_1": cc})
            copy.start()
            sends.append(copy)
    answers_in[me] = answers[15]

    pre = jnp.zeros((rows, part.shape[1]), F32)
    for d in (1, 3, 2):
        origin = lax.rem(y + 4 - d, 4)
        send(parts.at[0], parts_in.at[origin], rs.at[d - 1], rr.at[d - 1],
             {"chan": origin}).wait_recv()
        pre = pre + parts_in[origin].astype(F32)
    pre = pre + parts[y].astype(F32)
    sigma = 1.0 / (1.0 + jnp.exp(-pre))
    result[pl.ds(0, rows), :] = columns[:, 1:2] * (sigma * (1.0 + pre * (1.0 - sigma)))
    slots = 16 * CAP
    chosen = one_hot(
        jnp.broadcast_to(columns[:, 0:1], (rows, slots)) == iota((rows, slots), 1).astype(F32)
    )
    for k in range(15):
        zz, cc = pair(k, True)
        send(answers.at[0], answers_in.at[zz * 2 + cc], ans_s.at[k], ans_r.at[k],
             {"pix_0": zz, "pix_1": cc}).wait_recv()
    rows_in = answers_in[...].reshape(slots, part.shape[1])
    fetched = jnp.dot(chosen, rows_in, preferred_element_type=F32)
    part[...] = (result[pl.ds(0, rows), :] * fetched).astype(BF16)

    sends += gather_multiply(part, spec, shards, total, gs, gr)
    sends += add_up(total, result, half_out, half_in, turned, xs, xr, zf, zs, zr, pieces, sems)
    out[...] = result[...].astype(out.dtype)
    for copy in sends:
        copy.wait_send()


def shards(spectra, enc_weight, pix_tile, pix_local, foot_weight, cotangent, adjoint, mixing):
    rows, features = spectra.shape[0] // 4, cotangent.shape[1]
    channels = spectra.shape[1]
    dma = pltpu.SemaphoreType.DMA
    vmem = pl.BlockSpec(memory_space=pltpu.VMEM)
    anywhere = pl.BlockSpec(memory_space=pl.ANY)
    half, line, wide = features // 2, channels // 4, channels // 32
    encoded = pl.pallas_call(
        whole_kernel,
        out_shape=jax.ShapeDtypeStruct((channels, features), BF16),
        in_specs=[anywhere, vmem, vmem, vmem, vmem, anywhere, vmem, vmem],
        out_specs=vmem,
        scratch_shapes=[
            pltpu.VMEM(spectra.shape, BF16),
            pltpu.VMEM((TILE + 256, features), BF16),
            pltpu.VMEM((TILE, features), BF16),
            pltpu.VMEM((4, rows, features), BF16),
            pltpu.VMEM((4, rows, features), BF16),
            pltpu.VMEM((16, 1, 128), F32),
            pltpu.VMEM((16, 1, 128), F32),
            pltpu.VMEM((128, 128), F32),
            pltpu.VMEM((rows, 128), F32),
            pltpu.VMEM((16, CAP, features), BF16),
            pltpu.VMEM((16, CAP, features), BF16),
            pltpu.VMEM((rows, features), BF16),
            pltpu.VMEM((4, rows, features), BF16),
            pltpu.VMEM((features, channels), F32),
            pltpu.VMEM((half, channels), BF16),
            pltpu.VMEM((half, channels), BF16),
            pltpu.VMEM((channels, half), F32),
            pltpu.VMEM((4, line, half), BF16),
            pltpu.VMEM((4, line, half), BF16),
            pltpu.VMEM((8, wide, half), F32),
            pltpu.VMEM((8, wide, half), BF16),
            pltpu.VMEM((8, wide, half), BF16),
            pltpu.VMEM((2, 4, 8, wide, half), BF16),
            pltpu.VMEM((channels, features), F32),
        ]
        + [
            dma(shape)
            for shape in [(4,), ()]
            + [(n,) for n in (2, 2, 15, 15, 15, 15, 3, 3, 6, 6)]
            + [(), ()]
            + [(n,) for n in (3, 3, 7, 7, 7, 7, 24, 24, 4, 4)]
        ],
        compiler_params=pltpu.CompilerParams(collective_id=0, has_side_effects=True),
        name="whole",
    )(
        spectra,
        enc_weight,
        pix_tile.reshape(16, 128),
        pix_local.reshape(16, 128),
        foot_weight.reshape(16, 128),
        cotangent,
        adjoint,
        mixing,
    )
    return encoded.astype(F32)


def solution(mesh):
    finer = Mesh(
        mesh.devices.reshape(mesh.shape["obs"], 8, 2, mesh.shape["chan"]),
        ("obs", "pix_0", "pix_1", "chan"),
    )
    placed = (
        P(OBS_PIX, "chan"),
        P("chan", None),
        P(OBS_PIX, None),
        P(OBS_PIX),
        P(OBS_PIX),
        P(PIX, None),
        P(None, PIX),
        P(),
    )
    return jax.shard_map(
        shards, mesh=finer, in_specs=placed, out_specs=P("chan", None), check_vma=False
    )
```

time: 150 us -> 86.2 us (0.57)
  Pallas kernels: 42.1 us -> 83.9 us
  matrix products: 31.6 us -> 0 us
  starting transfers between devices: 28.5 us -> 0 us
  other arithmetic: 17.4 us -> 2.16 us
  waiting for transfers between devices: 15 us -> 0 us
  local copies, waits for them, and re-layouts: 14.8 us -> 0 us
    pallas_call x1, Pallas kernels: 42.1 us -> 83.9 us  [shards(): pl.pallas_call(whole_kernel, out_shape=jax.ShapeDtypeStruct((channels, fe...]
    dot_general x9 -> x0, matrix products: 31.6 us -> none  [the longest x8 26.6 us: shards(): jnp.einsum('bij,bje->bie', selector, windows, preferred_element_type=jnp....]
    all_to_all x3 -> x0, starting transfers between devices: 21.6 us -> none  [the longest x1 9.9 us: fetch_rows(): lax.all_to_all(outgoing, PIX, split_axis=0, concat_axis=0, tiled=True)]
    all_to_all x3 -> x0, waiting for transfers between devices: 15 us -> none  [the longest x1 15 us: fetch_rows(): lax.all_to_all(fetched, PIX, split_axis=0, concat_axis=0, tiled=True)]
    convert_element_type x3 -> x1, other arithmetic: 10.6 us -> 2.16 us  [shards(): return encoded.astype(F32)]
    ppermute x2 -> x0, starting transfers between devices: 6.84 us -> none  [the longest x1 4.92 us: extended(): before = lax.ppermute(last, axis, up)]
    gather x2 -> x0, local copies, waits for them, and re-layouts: 5.89 us -> none  [the longest x1 3.94 us: fetch_rows(): fetched = jnp.take(pixel_grad, jnp.where(usable, requested, 0), axis=0)]
    scatter x1 -> x0, local copies, waits for them, and re-layouts: 2.44 us -> none  [fetch_rows(): jnp.full((tile_count * capacity,), -1, jnp.int32).at[slot_index]]
  transfers between devices with their start and end apart: 5 -> 0, of which waited for: 1 -> 0; matrix products, arithmetic and copies ran while one was open for 38% -> 0% of each run, Pallas kernels for 0% -> 0%
where the time goes in v2:
time: 86.2 us; the launch traced here: 86.1 us
  Pallas kernels  83.9 us (97%)
  other arithmetic  2.16 us (3%)
    pallas_call x1, Pallas kernels, shards(): pl.pallas_call(whole_kernel, out_shape=jax.ShapeDtypeStruct((channels, fe...  83.9 us
    convert_element_type x1, other arithmetic, shards(): return encoded.astype(F32)  2.16 us

profile of v2, /device:TPU:1, one launch (start us, length us, event | category | flops | bytes accessed | tf_op | source)
XLA Modules:
  0.0 86.1 jit_solution(2849727179242854410)
XLA Ops:
  0.0 83.9 %whole.1 = bf16[1152,256]{1,0:T(8,128)(2,1)} custom-call(bf16[2048,1152]{1,0:T(8,128)(2,1)} %spec_hbm.1, bf16[1152,256]{1,0:T(8,128)(2,1)} %weight.1, s32[16,128]{1,0:T(8,128)} %bitcast.3, s32[16,128]{1,0:T(8,128)} %bitcast.4, f32[16,128]{1,0:T(8,128)} %bitcast.5, bf16[4096,256]{1,0:T(8,128)(2,1)} %cot_hbm.1, s32[8,4096]{1,0:T(8,128)} %adjoint.1, ...), custom_call_target="tpu_custom_call" | custom-call | tf_op jit(solution)/shard_map/whole/pallas_call | solution.py:374
  83.9 2.2 %convert_element_type.3 = f32[1152,256]{1,0:T(8,128)} convert(bf16[1152,256]{1,0:T(8,128)(2,1)} %whole.1) | non-fusion elementwise | flops 294912 | bytes 1769472 | tf_op jit(solution)/shard_map/convert_element_type | solution.py:424

commit v3 on v0

v3 whole, which is shorter than its diff:
```python
import jax
import jax.numpy as jnp
from jax import lax
from jax.experimental import pallas as pl
from jax.experimental.pallas import tpu as pltpu
from jax.sharding import Mesh
from jax.sharding import PartitionSpec as P

TILE = 4096
CAP = 64
SIDE = 128
STEPS = (4, 3, 5, 2, 6, 1, 7, 0)
PIX = ("pix_0", "pix_1")
OBS_PIX = ("obs", "pix_0", "pix_1")
AXES = ("obs", "pix_0", "pix_1", "chan")
BF16 = jnp.bfloat16
F32 = jnp.float32


def send(source, target, send_sem, recv_sem, where):
    return pltpu.make_async_remote_copy(
        src_ref=source,
        dst_ref=target,
        send_sem=send_sem,
        recv_sem=recv_sem,
        device_id=where,
        device_id_type=pl.DeviceIdType.MESH,
    )


def greet():
    barrier = pltpu.get_barrier_semaphore()
    x, z, c, y = (lax.axis_index(name) for name in AXES)
    peers = [{"obs": lax.rem(x + d, 4)} for d in range(1, 4)]
    peers += [{"chan": lax.rem(y + d, 4)} for d in range(1, 4)]
    for d in range(8):
        for e in range(2):
            if d or e:
                peers.append({"pix_0": lax.rem(z + d, 8), "pix_1": lax.rem(c + e, 2)})
    for peer in peers:
        pl.semaphore_signal(
            barrier, inc=1, device_id=peer, device_id_type=pl.DeviceIdType.MESH
        )
    return barrier, len(peers)


def one_hot(condition):
    return jnp.where(condition, 1.0, 0.0).astype(BF16)


def iota(shape, dim):
    return lax.broadcasted_iota(jnp.int32, shape, dim)


def own_rows(ref, y):
    return jnp.concatenate([ref[pl.ds(4 * y + j, 1), :] for j in range(4)], axis=1)


def ask(tile, local, weight, y, asked, columns):
    tiles, locals_, weights = own_rows(tile, y), own_rows(local, y), own_rows(weight, y)
    rows = tiles.shape[1]
    named = jnp.broadcast_to(tiles, (16, rows)) == iota((16, rows), 0)
    earlier = one_hot(iota((rows, rows), 0) < iota((rows, rows), 1))
    counts = jnp.dot(one_hot(named), earlier, preferred_element_type=F32)
    rank = jnp.sum(jnp.where(named, counts, 0.0), axis=0, keepdims=True)
    placed = one_hot(jnp.broadcast_to(rank, (128, rows)) == iota((128, rows), 0).astype(F32))
    high = lax.shift_right_logical(locals_, 6)
    low = locals_ - high * 64
    wanted = jnp.zeros((16, 128), F32)
    for digit, scale in ((high, 64.0), (low, 1.0)):
        held = jnp.where(named, jnp.broadcast_to(digit.astype(F32), (16, rows)), 0.0).astype(BF16)
        wanted += scale * lax.dot_general(
            held, placed, (((1,), (1,)), ((), ())), preferred_element_type=F32
        )
    for t in range(16):
        asked[t] = wanted[t : t + 1, :]
    slot = tiles.astype(F32) * CAP + rank
    both = jnp.where(iota((128, rows), 0) == 0, jnp.broadcast_to(slot, (128, rows)),
                     jnp.broadcast_to(weights, (128, rows)))
    for j in range(rows // 128):
        block = pl.ds(j * 128, 128)
        columns[block, :] = jnp.transpose(both[:, j * 128 : (j + 1) * 128])


def pixel_block(b, cot, adjoint, mixing, table, tile):
    block = SIDE
    lanes = iota((block, 3 * block), 1).astype(F32)
    start = pl.multiple_of(b * block, block)
    first = tile * TILE + start - block
    within = jnp.transpose((adjoint[:, pl.ds(start, block)] - first).astype(F32))
    window = cot[pl.ds(start, 3 * block), :]
    wide = (block, window.shape[1])
    ahead = jnp.broadcast_to(within[:, 0:1], wide) - iota(wide, 0).astype(F32) > 128.0
    edge = jnp.where(ahead, window[2 * block :].astype(F32), window[:block].astype(F32))
    total = window[block : 2 * block].astype(F32) + edge * mixing[pl.ds(0, 1), :]
    for k in range(1, 8):
        chosen = one_hot(jnp.broadcast_to(within[:, k : k + 1], lanes.shape) == lanes)
        picked = jnp.dot(chosen, window, preferred_element_type=F32)
        total = total + picked * mixing[pl.ds(k, 1), :]
    table[pl.ds(start, block), :] = total.astype(BF16)


def answer(requests, table, start, answers):
    step = 512
    wanted = jnp.concatenate(
        [requests[0:CAP, k : k + 1] for k in range(start, start + 8)], axis=0
    )
    wanted = jnp.broadcast_to(wanted, (8 * CAP, step))
    lanes = iota((8 * CAP, step), 1).astype(F32)
    total = jnp.zeros((8 * CAP, table.shape[1]), F32)
    for j in range(TILE // step):
        chosen = one_hot(wanted - float(j * step) == lanes)
        total += jnp.dot(chosen, table[pl.ds(j * step, step), :], preferred_element_type=F32)
    for k in range(8):
        for h in range(2):
            rows = total[k * CAP : (k + 1) * CAP, h * SIDE : (h + 1) * SIDE]
            answers[h, start + k] = rows.astype(BF16)


def whole_kernel(spec_hbm, weight, tile, local, foot, cot_hbm, adjoint, mixing, out, spec, cot,
                 table, parts, parts_in, relay, asked, asked_in, square, columns, answers,
                 answers_in, slope, chosen, part, shards, total, turned, cs, cr, mine, xs, xr,
                 xsum, zf, zs, zr, pieces, result, load_sems, cot_sem, halo_s, halo_r, ask_s,
                 ask_r, ans_s, ans_r, rs, rr, gs, gr, core_s, core_r, xs_s, xs_r, zs_s, zs_r,
                 pz_s, pz_r, px_s, px_r, pc_s, pc_r):
    x, z, c, y = (lax.axis_index(name) for name in AXES)
    o = 1 - c
    me = z * 2 + c
    rows = part.shape[1]
    right, left, far = lax.rem(y + 1, 4), lax.rem(y + 3, 4), lax.rem(y + 2, 4)
    to_right, to_left = {"chan": right}, {"chan": left}
    lo, hi = pl.ds(0, rows // 2), pl.ds(rows // 2, rows // 2)
    near = (1, 3, 2)
    ring = (1, 7, 2, 6, 3, 5, 4)
    sends = []

    def go(*args):
        copy = send(*args)
        copy.start()
        sends.append(copy)

    def arrived(*args):
        send(*args).wait_recv()

    barrier, count = greet()
    cot_copy = pltpu.make_async_copy(cot_hbm, cot.at[pl.ds(128, TILE)], cot_sem)
    cot_copy.start()
    owners = (far, right, left, y)
    spec_copies = []
    for step, owner in enumerate(owners):
        block = pl.ds(pl.multiple_of(owner * rows, rows), rows)
        copy = pltpu.make_async_copy(spec_hbm.at[block], spec.at[block], load_sems.at[step])
        copy.start()
        spec_copies.append(copy)
    ask(tile, local, foot, y, asked, columns)
    cot_copy.wait()

    order = [(d, e) for d in STEPS for e in (1, 0)]

    def pair(k, ahead):
        d, e = order[k]
        return lax.rem(z + (d if ahead else 8 - d), 8), lax.rem(c + e, 2)

    def pixels(step):
        owner = owners[step]

        def group(i, carry):
            for j in range(4):
                b = lax.rem(8 * step + 4 * i + j + 1, TILE // SIDE)
                pixel_block(b, cot, adjoint, mixing, table, me)
            half = pl.multiple_of(i * (rows // 2), rows // 2)
            block = spec[pl.ds(pl.multiple_of(owner * rows + half, rows // 2), rows // 2), :]
            product = jnp.dot(block, weight[...], preferred_element_type=F32)
            parts[owner, pl.ds(half, rows // 2), :] = product.astype(BF16)
            return carry

        spec_copies[step].wait()
        lax.fori_loop(0, 2, group, 0)

    after = {"pix_0": lax.rem(z + c, 8), "pix_1": o}
    before = {"pix_0": lax.rem(z + 7 + c, 8), "pix_1": o}
    pixels(0)
    pl.semaphore_wait(barrier, count)
    for k in range(15):
        zz, cc = pair(k, True)
        go(asked.at[zz * 2 + cc], asked_in.at[me], ask_s.at[k], ask_r.at[k],
           {"pix_0": zz, "pix_1": cc})
    ends = cot.at[pl.ds(0, 128)], cot.at[pl.ds(TILE + 128, 128)]
    go(cot_hbm.at[pl.ds(0, 128)], ends[1], halo_s.at[0], halo_r.at[0], before)
    go(cot_hbm.at[pl.ds(TILE - 128, 128)], ends[0], halo_s.at[1], halo_r.at[1], after)
    go(parts.at[far, lo], relay.at[0], rs.at[0], rr.at[0], to_right)
    go(parts.at[far, hi], relay.at[1], rs.at[1], rr.at[1], to_left)
    pixels(1)
    go(parts.at[right], parts_in.at[y], rs.at[2], rr.at[2], to_right)
    pixels(2)
    go(parts.at[left], parts_in.at[y], rs.at[3], rr.at[3], to_left)
    arrived(parts.at[far, lo], relay.at[0], rs.at[0], rr.at[0], to_left)
    go(relay.at[0], parts_in.at[left, lo], rs.at[4], rr.at[4], to_right)
    arrived(parts.at[far, hi], relay.at[1], rs.at[1], rr.at[1], to_right)
    go(relay.at[1], parts_in.at[right, hi], rs.at[5], rr.at[5], to_left)
    arrived(cot_hbm.at[pl.ds(0, 128)], ends[1], halo_s.at[0], halo_r.at[0], after)
    arrived(cot_hbm.at[pl.ds(0, 128)], ends[0], halo_s.at[1], halo_r.at[1], before)
    pixels(3)

    square[...] = jnp.zeros_like(square)
    for k in range(15):
        zz, cc = pair(k, False)
        arrived(asked.at[0], asked_in.at[zz * 2 + cc], ask_s.at[k], ask_r.at[k],
                {"pix_0": zz, "pix_1": cc})
        square[pl.ds(k, 1), :] = asked_in[zz * 2 + cc]
    square[pl.ds(15, 1), :] = asked[me]
    requests = jnp.transpose(square[...])

    def reply(h, first, last):
        for k in range(first, last):
            zz, cc = pair(k, False)
            go(answers.at[h, k], answers_in.at[h, me], ans_s.at[h * 15 + k],
               ans_r.at[h * 15 + k], {"pix_0": zz, "pix_1": cc})

    answer(requests, table, 0, answers)
    reply(0, 0, 8)
    answer(requests, table, 8, answers)
    reply(0, 8, 15)
    reply(1, 0, 15)
    for h in range(2):
        answers_in[h, me] = answers[h, 15]

    slots = 16 * CAP
    chosen[...] = one_hot(
        jnp.broadcast_to(columns[:, 0:1], (rows, slots)) == iota((rows, slots), 1).astype(F32)
    )
    arrived(parts.at[0], parts_in.at[left], rs.at[2], rr.at[2], to_left)
    arrived(parts.at[0], parts_in.at[right], rs.at[3], rr.at[3], to_right)
    arrived(relay.at[0], parts_in.at[far, lo], rs.at[4], rr.at[4], to_left)
    arrived(relay.at[1], parts_in.at[far, hi], rs.at[5], rr.at[5], to_right)
    pre = parts[y].astype(F32)
    for origin in (left, right, far):
        pre = pre + parts_in[origin].astype(F32)
    sigma = 1.0 / (1.0 + jnp.exp(-pre))
    slope[...] = columns[:, 1:2] * (sigma * (1.0 + pre * (1.0 - sigma)))

    def fetch(h):
        for k in range(15):
            zz, cc = pair(k, True)
            arrived(answers.at[h, k], answers_in.at[h, zz * 2 + cc], ans_s.at[h * 15 + k],
                    ans_r.at[h * 15 + k], {"pix_0": zz, "pix_1": cc})
        rows_in = answers_in[h].reshape(slots, SIDE)
        fetched = jnp.dot(chosen[...], rows_in, preferred_element_type=F32)
        part[h] = (slope[:, h * SIDE : (h + 1) * SIDE] * fetched).astype(BF16)

    def multiply(h, gradient, owner, fresh=False):
        flat = jnp.transpose(gradient.astype(F32)).astype(BF16)
        width = spec.shape[1] // 3
        for n in range(3):
            cols = pl.ds(n * width, width)
            block = spec[pl.ds(pl.multiple_of(owner * rows, rows), rows), cols]
            product = jnp.dot(flat, block, preferred_element_type=F32)
            if fresh:
                total[h, :, cols] = product
            else:
                total[h, :, cols] += product

    def gather_start(h):
        i = h * 6
        mine_, store = part.at[h], shards.at[h]
        go(mine_.at[lo], store.at[y, lo], gs.at[i], gr.at[i], to_right)
        go(mine_.at[hi], store.at[y, hi], gs.at[i + 1], gr.at[i + 1], to_left)
        go(mine_.at[hi], store.at[y, hi], gs.at[i + 2], gr.at[i + 2], to_right)
        go(mine_.at[lo], store.at[y, lo], gs.at[i + 3], gr.at[i + 3], to_left)
        multiply(h, part[h], y, True)

    def gather_near(h):
        i = h * 6
        mine_, store = part.at[h], shards.at[h]
        arrived(mine_.at[lo], store.at[left, lo], gs.at[i], gr.at[i], to_left)
        go(store.at[left, lo], store.at[left, lo], gs.at[i + 4], gr.at[i + 4], to_right)
        arrived(mine_.at[hi], store.at[right, hi], gs.at[i + 1], gr.at[i + 1], to_right)
        go(store.at[right, hi], store.at[right, hi], gs.at[i + 5], gr.at[i + 5], to_left)
        arrived(mine_.at[hi], store.at[left, hi], gs.at[i + 2], gr.at[i + 2], to_left)
        multiply(h, shards[h, left], left)
        arrived(mine_.at[lo], store.at[right, lo], gs.at[i + 3], gr.at[i + 3], to_right)
        multiply(h, shards[h, right], right)

    core_lines, line, wide = mine.shape[1], xs.shape[2], zs.shape[2]

    def gather_far(h):
        i = h * 6
        store = shards.at[h]
        arrived(store.at[far, lo], store.at[far, lo], gs.at[i + 4], gr.at[i + 4], to_left)
        arrived(store.at[far, hi], store.at[far, hi], gs.at[i + 5], gr.at[i + 5], to_right)
        multiply(h, shards[h, far], far)
        for j in range(total.shape[2] // SIDE):
            block = pl.ds(j * SIDE, SIDE)
            turned[h, block, :] = jnp.transpose(total[h, :, block])
        theirs = pl.ds(pl.multiple_of(o * core_lines, 8), core_lines)
        cs[h] = turned[h, theirs, :].astype(BF16)
        go(cs.at[h], cr.at[h], core_s.at[h], core_r.at[h], {"pix_1": o})

    def core_sum(h):
        arrived(cs.at[h], cr.at[h], core_s.at[h], core_r.at[h], {"pix_1": o})
        ours = pl.ds(pl.multiple_of(c * core_lines, 8), core_lines)
        mine[h] = turned[h, ours, :] + cr[h].astype(F32)
        for j in range(4):
            xs[h, j] = mine[h, pl.ds(j * line, line), :].astype(BF16)
        for d in near:
            peer = lax.rem(x + d, 4)
            at = h * 3 + d - 1
            go(xs.at[h, peer], xr.at[h, x], xs_s.at[at], xs_r.at[at], {"obs": peer})

    def x_sum(h):
        summed = mine[h, pl.ds(pl.multiple_of(x * line, 8), line), :]
        for d in near:
            origin = lax.rem(x + 4 - d, 4)
            at = h * 3 + d - 1
            arrived(xs.at[h, 0], xr.at[h, origin], xs_s.at[at], xs_r.at[at], {"obs": origin})
            summed = summed + xr[h, origin].astype(F32)
        xsum[h] = summed
        for j in range(8):
            zf[h, j] = xsum[h, pl.ds(j * wide, wide), :]
            zs[h, j] = zf[h, j].astype(BF16)
        for d in ring:
            peer = lax.rem(z + d, 8)
            at = h * 7 + d - 1
            go(zs.at[h, peer], zr.at[h, z], zs_s.at[at], zs_r.at[at], {"pix_0": peer})

    def z_sum(h):
        own = zf[h, z]
        for d in ring:
            origin = lax.rem(z + 8 - d, 8)
            at = h * 7 + d - 1
            arrived(zs.at[h, 0], zr.at[h, origin], zs_s.at[at], zs_r.at[at], {"pix_0": origin})
            own = own + zr[h, origin].astype(F32)
        pieces[h, c, x, z] = own.astype(BF16)
        piece = pieces.at[h, c, x, z]
        for d in ring:
            at = h * 7 + d - 1
            go(piece, piece, pz_s.at[at], pz_r.at[at], {"pix_0": lax.rem(z + d, 8)})

    def z_gather(h):
        for d in (0,) + ring:
            origin = lax.rem(z + 8 - d, 8)
            piece = pieces.at[h, c, x, origin]
            if d:
                at = h * 7 + d - 1
                arrived(piece, piece, pz_s.at[at], pz_r.at[at], {"pix_0": origin})
            for e in near:
                at = (h * 8 + d) * 3 + e - 1
                go(piece, piece, px_s.at[at], px_r.at[at], {"obs": lax.rem(x + e, 4)})
        group = pieces.at[h, c, x]
        go(group, group, pc_s.at[h * 4], pc_r.at[h * 4], {"pix_1": o})

    def x_gather(h):
        for e in near:
            column = lax.rem(x + 4 - e, 4)
            for d in (0,) + ring:
                at = (h * 8 + d) * 3 + e - 1
                piece = pieces.at[h, c, column, lax.rem(z + 8 - d, 8)]
                arrived(piece, piece, px_s.at[at], px_r.at[at], {"obs": column})
            group = pieces.at[h, c, column]
            go(group, group, pc_s.at[h * 4 + e], pc_r.at[h * 4 + e], {"pix_1": o})

    def core_gather(h):
        for e in (0,) + near:
            group = pieces.at[h, o, lax.rem(x + 4 - e, 4)]
            arrived(group, group, pc_s.at[h * 4 + e], pc_r.at[h * 4 + e], {"pix_1": o})
        for cc in range(2):
            for xx in range(4):
                for zz in range(8):
                    row = cc * core_lines + xx * line + zz * wide
                    result[pl.ds(row, wide), :] = pieces[h, cc, xx, zz].astype(F32)
        out[:, h * SIDE : (h + 1) * SIDE] = result[...].astype(out.dtype)

    fetch(0)
    gather_start(0)
    gather_near(0)
    fetch(1)
    gather_start(1)
    gather_far(0)
    gather_near(1)
    core_sum(0)
    gather_far(1)
    x_sum(0)
    core_sum(1)
    z_sum(0)
    x_sum(1)
    z_gather(0)
    z_sum(1)
    x_gather(0)
    z_gather(1)
    core_gather(0)
    x_gather(1)
    core_gather(1)
    for copy in sends:
        copy.wait_send()


def shards(spectra, enc_weight, pix_tile, pix_local, foot_weight, cotangent, adjoint, mixing):
    rows, features = spectra.shape[0] // 4, cotangent.shape[1]
    channels = spectra.shape[1]
    dma = pltpu.SemaphoreType.DMA
    vmem = pl.BlockSpec(memory_space=pltpu.VMEM)
    anywhere = pl.BlockSpec(memory_space=pl.ANY)
    core, line, wide = channels // 2, channels // 8, channels // 64
    shapes = [
        (spectra.shape, BF16),
        ((TILE + 256, features), BF16),
        ((TILE, features), BF16),
        ((4, rows, features), BF16),
        ((4, rows, features), BF16),
        ((2, rows // 2, features), BF16),
        ((16, 1, 128), F32),
        ((16, 1, 128), F32),
        ((128, 128), F32),
        ((rows, 128), F32),
        ((2, 16, CAP, SIDE), BF16),
        ((2, 16, CAP, SIDE), BF16),
        ((rows, features), F32),
        ((rows, 16 * CAP), BF16),
        ((2, rows, SIDE), BF16),
        ((2, 4, rows, SIDE), BF16),
        ((2, SIDE, channels), F32),
        ((2, channels, SIDE), F32),
        ((2, core, SIDE), BF16),
        ((2, core, SIDE), BF16),
        ((2, core, SIDE), F32),
        ((2, 4, line, SIDE), BF16),
        ((2, 4, line, SIDE), BF16),
        ((2, line, SIDE), F32),
        ((2, 8, wide, SIDE), F32),
        ((2, 8, wide, SIDE), BF16),
        ((2, 8, wide, SIDE), BF16),
        ((2, 2, 4, 8, wide, SIDE), BF16),
        ((channels, SIDE), F32),
    ]
    counts = [2, 15, 30, 6, 12, 2, 6, 14, 14, 48, 8]
    encoded = pl.pallas_call(
        whole_kernel,
        out_shape=jax.ShapeDtypeStruct((channels, features), BF16),
        in_specs=[anywhere, vmem, vmem, vmem, vmem, anywhere, vmem, vmem],
        out_specs=vmem,
        scratch_shapes=[pltpu.VMEM(shape, kind) for shape, kind in shapes]
        + [dma((4,)), dma(())]
        + [dma((n,)) for n in counts for _ in range(2)],
        compiler_params=pltpu.CompilerParams(collective_id=0, has_side_effects=True),
        name="whole",
    )(
        spectra,
        enc_weight,
        pix_tile.reshape(16, 128),
        pix_local.reshape(16, 128),
        foot_weight.reshape(16, 128),
        cotangent,
        adjoint,
        mixing,
    )
    return encoded.astype(F32)


def solution(mesh):
    finer = Mesh(
        mesh.devices.reshape(mesh.shape["obs"], 8, 2, mesh.shape["chan"]),
        ("obs", "pix_0", "pix_1", "chan"),
    )
    placed = (
        P(OBS_PIX, "chan"),
        P("chan", None),
        P(OBS_PIX, None),
        P(OBS_PIX),
        P(OBS_PIX),
        P(PIX, None),
        P(None, PIX),
        P(),
    )
    return jax.shard_map(
        shards, mesh=finer, in_specs=placed, out_specs=P("chan", None), check_vma=False
    )
```

time: 199 us -> 80.1 us (0.40)
  blocking collectives: 85.8 us -> 0 us
  Pallas kernels: 0 us -> 77.8 us
  matrix products: 35.5 us -> 0 us
  starting transfers between devices: 28.5 us -> 0 us
  local copies, waits for them, and re-layouts: 16.4 us -> 0 us
  waiting for transfers between devices: 15 us -> 0 us
  other arithmetic: 16.9 us -> 2.16 us
    all_to_all x5 -> x0, blocking collectives: 85.8 us -> none  [the longest x3 56.7 us: copy_for_each(): lax.all_to_all(jnp.broadcast_to(value[None], (length, *value.shape)), axi...]
    pallas_call x0 -> x1, Pallas kernels: none -> 77.8 us  [shards(): pl.pallas_call(whole_kernel, out_shape=jax.ShapeDtypeStruct((channels, fe...]
    dot_general x10 -> x0, matrix products: 35.5 us -> none  [the longest x8 26.6 us: shards(): jnp.einsum('bij,bje->bie', selector, windows, preferred_element_type=jnp....]
    all_to_all x3 -> x0, starting transfers between devices: 21.6 us -> none  [the longest x1 9.9 us: fetch_rows(): lax.all_to_all(outgoing, PIX, split_axis=0, concat_axis=0, tiled=True)]
    all_to_all x3 -> x0, waiting for transfers between devices: 15 us -> none  [the longest x1 15 us: fetch_rows(): lax.all_to_all(fetched, PIX, split_axis=0, concat_axis=0, tiled=True)]
    convert_element_type x3 -> x1, other arithmetic: 9.91 us -> 2.16 us  [shards(): return encoded.astype(F32)]
    ppermute x2 -> x0, starting transfers between devices: 6.84 us -> none  [the longest x1 4.92 us: extended(): before = lax.ppermute(last, axis, up)]
    gather x2 -> x0, local copies, waits for them, and re-layouts: 5.89 us -> none  [the longest x1 3.94 us: fetch_rows(): fetched = jnp.take(pixel_grad, jnp.where(usable, requested, 0), axis=0)]
  transfers between devices with their start and end apart: 5 -> 0, of which waited for: 1 -> 0; matrix products, arithmetic and copies ran while one was open for 29% -> 0% of each run, Pallas kernels for 0% -> 0%
where the time goes in v3:
time: 80.1 us; the launch traced here: 79.9 us
  Pallas kernels  77.8 us (97%)
  other arithmetic  2.16 us (3%)
    pallas_call x1, Pallas kernels, shards(): pl.pallas_call(whole_kernel, out_shape=jax.ShapeDtypeStruct((channels, fe...  77.8 us
    convert_element_type x1, other arithmetic, shards(): return encoded.astype(F32)  2.16 us

profile of v3, /device:TPU:1, one launch (start us, length us, event | category | flops | bytes accessed | tf_op | source)
XLA Modules:
  0.0 79.9 jit_solution(10683582400036298121)
XLA Ops:
  0.0 77.8 %whole.1 = bf16[1152,256]{1,0:T(8,128)(2,1)} custom-call(bf16[2048,1152]{1,0:T(8,128)(2,1)} %spec_hbm.1, bf16[1152,256]{1,0:T(8,128)(2,1)} %weight.1, s32[16,128]{1,0:T(8,128)} %bitcast.3, s32[16,128]{1,0:T(8,128)} %bitcast.4, f32[16,128]{1,0:T(8,128)} %bitcast.5, bf16[4096,256]{1,0:T(8,128)(2,1)} %cot_hbm.1, s32[8,4096]{1,0:T(8,128)} %adjoint.1, ...), custom_call_target="tpu_custom_call" | custom-call | tf_op jit(solution)/shard_map/whole/pallas_call | solution.py:436
  77.8 2.2 %convert_element_type.3 = f32[1152,256]{1,0:T(8,128)} convert(bf16[1152,256]{1,0:T(8,128)(2,1)} %whole.1) | non-fusion elementwise | flops 294912 | bytes 1769472 | tf_op jit(solution)/shard_map/convert_element_type | solution.py:456

commit v4 on v3

--- a/solution.py
+++ b/solution.py
@@ -73,7 +73,7 @@
             held, placed, (((1,), (1,)), ((), ())), preferred_element_type=F32
         )
     for t in range(16):
-        asked[t] = wanted[t : t + 1, :]
+        asked[t] = jnp.clip(wanted[t : t + 1, :].astype(jnp.int32), 0, TILE - 1)
     slot = tiles.astype(F32) * CAP + rank
     both = jnp.where(iota((128, rows), 0) == 0, jnp.broadcast_to(slot, (128, rows)),
                      jnp.broadcast_to(weights, (128, rows)))
@@ -82,47 +82,21 @@
         columns[block, :] = jnp.transpose(both[:, j * 128 : (j + 1) * 128])
 
 
-def pixel_block(b, cot, adjoint, mixing, table, tile):
-    block = SIDE
-    lanes = iota((block, 3 * block), 1).astype(F32)
-    start = pl.multiple_of(b * block, block)
-    first = tile * TILE + start - block
-    within = jnp.transpose((adjoint[:, pl.ds(start, block)] - first).astype(F32))
-    window = cot[pl.ds(start, 3 * block), :]
-    wide = (block, window.shape[1])
-    ahead = jnp.broadcast_to(within[:, 0:1], wide) - iota(wide, 0).astype(F32) > 128.0
-    edge = jnp.where(ahead, window[2 * block :].astype(F32), window[:block].astype(F32))
-    total = window[block : 2 * block].astype(F32) + edge * mixing[pl.ds(0, 1), :]
-    for k in range(1, 8):
-        chosen = one_hot(jnp.broadcast_to(within[:, k : k + 1], lanes.shape) == lanes)
-        picked = jnp.dot(chosen, window, preferred_element_type=F32)
-        total = total + picked * mixing[pl.ds(k, 1), :]
-    table[pl.ds(start, block), :] = total.astype(BF16)
-
-
-def answer(requests, table, start, answers):
-    step = 512
-    wanted = jnp.concatenate(
-        [requests[0:CAP, k : k + 1] for k in range(start, start + 8)], axis=0
-    )
-    wanted = jnp.broadcast_to(wanted, (8 * CAP, step))
-    lanes = iota((8 * CAP, step), 1).astype(F32)
-    total = jnp.zeros((8 * CAP, table.shape[1]), F32)
-    for j in range(TILE // step):
-        chosen = one_hot(wanted - float(j * step) == lanes)
-        total += jnp.dot(chosen, table[pl.ds(j * step, step), :], preferred_element_type=F32)
-    for k in range(8):
-        for h in range(2):
-            rows = total[k * CAP : (k + 1) * CAP, h * SIDE : (h + 1) * SIDE]
-            answers[h, start + k] = rows.astype(BF16)
-
-
-def whole_kernel(spec_hbm, weight, tile, local, foot, cot_hbm, adjoint, mixing, out, spec, cot,
-                 table, parts, parts_in, relay, asked, asked_in, square, columns, answers,
-                 answers_in, slope, chosen, part, shards, total, turned, cs, cr, mine, xs, xr,
-                 xsum, zf, zs, zr, pieces, result, load_sems, cot_sem, halo_s, halo_r, ask_s,
-                 ask_r, ans_s, ans_r, rs, rr, gs, gr, core_s, core_r, xs_s, xs_r, zs_s, zs_r,
-                 pz_s, pz_r, px_s, px_r, pc_s, pc_r):
+def widen(cot, rows_of, first, count):
+    for h in range(2):
+        half = cot[pl.ds(first, count), h * SIDE : (h + 1) * SIDE].astype(F32)
+        rows_of[pl.ds(2 * first + h, count, stride=2), :] = half
+
+
+def whole_kernel(spec_hbm, weight_hbm, tile_hbm, local_hbm, foot_hbm, cot_hbm, adjoint_hbm,
+                 mixing_hbm, out, weight, tile, local, foot, adjoint, mixing, spec, cot, rows_of, mixed, near_rows, formed, parts, parts_in, relay, asked, asked_in,
+                 wanted, chip_wanted, *rest):
+    lists, rest = rest[:8], rest[8:]
+    (columns, answers, answers_in, slope, chosen, part, shards, total, turned, cs, cr, mine, xs, xr,
+                 xsum, zf, zs, zr, pieces, result, load_sems, cot_sem, list_sems, want_sem,
+     chip_sem, in_sems,
+     halo_s, halo_r, ask_s, ask_r, ans_s, ans_r, rs, rr, gs, gr, core_s, core_r, xs_s, xs_r, zs_s,
+     zs_r, pz_s, pz_r, px_s, px_r, pc_s, pc_r) = rest
     x, z, c, y = (lax.axis_index(name) for name in AXES)
     o = 1 - c
     me = z * 2 + c
@@ -143,8 +117,26 @@
         send(*args).wait_recv()
 
     barrier, count = greet()
+    operands = ((adjoint_hbm, adjoint), (tile_hbm, tile), (local_hbm, local), (foot_hbm, foot),
+                (mixing_hbm, mixing), (weight_hbm, weight))
+    loads = [pltpu.make_async_copy(a, b, in_sems.at[i]) for i, (a, b) in enumerate(operands)]
+    for copy in loads[:5]:
+        copy.start()
     cot_copy = pltpu.make_async_copy(cot_hbm, cot.at[pl.ds(128, TILE)], cot_sem)
     cot_copy.start()
+    loads[5].start()
+    loads[0].wait()
+    inside = jnp.clip(adjoint[...] - (me * TILE - SIDE), 0, TILE + 2 * SIDE - 1)
+    near_rows[...] = inside * 2
+    list_copies = []
+    for k in range(8):
+        copy = pltpu.make_async_copy(near_rows.at[pl.ds(k, 1)], lists[k], list_sems.at[k])
+        copy.start()
+        list_copies.append(copy)
+    for copy in loads[1:5]:
+        copy.wait()
+    ask(tile, local, foot, y, asked, columns)
+    asked_in[me] = asked[me]
     owners = (far, right, left, y)
     spec_copies = []
     for step, owner in enumerate(owners):
@@ -152,8 +144,9 @@
         copy = pltpu.make_async_copy(spec_hbm.at[block], spec.at[block], load_sems.at[step])
         copy.start()
         spec_copies.append(copy)
-    ask(tile, local, foot, y, asked, columns)
-    cot_copy.wait()
+    for k in range(8):
+        for h in range(2):
+            mixed[pl.ds(2 * k + h, 1), :] = mixing[pl.ds(k, 1), h * SIDE : (h + 1) * SIDE]
 
     order = [(d, e) for d in STEPS for e in (1, 0)]
 
@@ -161,69 +154,108 @@
         d, e = order[k]
         return lax.rem(z + (d if ahead else 8 - d), 8), lax.rem(c + e, 2)
 
-    def pixels(step):
-        owner = owners[step]
-
-        def group(i, carry):
-            for j in range(4):
-                b = lax.rem(8 * step + 4 * i + j + 1, TILE // SIDE)
-                pixel_block(b, cot, adjoint, mixing, table, me)
-            half = pl.multiple_of(i * (rows // 2), rows // 2)
-            block = spec[pl.ds(pl.multiple_of(owner * rows + half, rows // 2), rows // 2), :]
-            product = jnp.dot(block, weight[...], preferred_element_type=F32)
-            parts[owner, pl.ds(half, rows // 2), :] = product.astype(BF16)
-            return carry
-
-        spec_copies[step].wait()
-        lax.fori_loop(0, 2, group, 0)
-
     after = {"pix_0": lax.rem(z + c, 8), "pix_1": o}
     before = {"pix_0": lax.rem(z + 7 + c, 8), "pix_1": o}
-    pixels(0)
     pl.semaphore_wait(barrier, count)
     for k in range(15):
         zz, cc = pair(k, True)
         go(asked.at[zz * 2 + cc], asked_in.at[me], ask_s.at[k], ask_r.at[k],
            {"pix_0": zz, "pix_1": cc})
-    ends = cot.at[pl.ds(0, 128)], cot.at[pl.ds(TILE + 128, 128)]
-    go(cot_hbm.at[pl.ds(0, 128)], ends[1], halo_s.at[0], halo_r.at[0], before)
-    go(cot_hbm.at[pl.ds(TILE - 128, 128)], ends[0], halo_s.at[1], halo_r.at[1], after)
+    ends = cot.at[pl.ds(0, SIDE)], cot.at[pl.ds(TILE + SIDE, SIDE)]
+    go(cot_hbm.at[pl.ds(0, SIDE)], ends[1], halo_s.at[0], halo_r.at[0], before)
+    go(cot_hbm.at[pl.ds(TILE - SIDE, SIDE)], ends[0], halo_s.at[1], halo_r.at[1], after)
+
+    cot_copy.wait()
+
+    def widen_step(i, carry):
+        widen(cot, rows_of, pl.multiple_of(SIDE + i * 256, SIDE), 256)
+        return carry
+
+    lax.fori_loop(0, TILE // 256, widen_step, 0)
+
+    loads[5].wait()
+
+    def encode(step):
+        owner = owners[step]
+        spec_copies[step].wait()
+        block = spec[pl.ds(pl.multiple_of(owner * rows, rows), rows), :]
+        parts[owner] = jnp.dot(block, weight[...], preferred_element_type=F32).astype(BF16)
+
+    encode(0)
     go(parts.at[far, lo], relay.at[0], rs.at[0], rr.at[0], to_right)
     go(parts.at[far, hi], relay.at[1], rs.at[1], rr.at[1], to_left)
-    pixels(1)
+    encode(1)
     go(parts.at[right], parts_in.at[y], rs.at[2], rr.at[2], to_right)
-    pixels(2)
+    encode(2)
     go(parts.at[left], parts_in.at[y], rs.at[3], rr.at[3], to_left)
-    arrived(parts.at[far, lo], relay.at[0], rs.at[0], rr.at[0], to_left)
-    go(relay.at[0], parts_in.at[left, lo], rs.at[4], rr.at[4], to_right)
-    arrived(parts.at[far, hi], relay.at[1], rs.at[1], rr.at[1], to_right)
-    go(relay.at[1], parts_in.at[right, hi], rs.at[5], rr.at[5], to_left)
-    arrived(cot_hbm.at[pl.ds(0, 128)], ends[1], halo_s.at[0], halo_r.at[0], after)
-    arrived(cot_hbm.at[pl.ds(0, 128)], ends[0], halo_s.at[1], halo_r.at[1], before)
-    pixels(3)
-
-    square[...] = jnp.zeros_like(square)
-    for k in range(15):
+    arrived(cot_hbm.at[pl.ds(0, SIDE)], ends[1], halo_s.at[0], halo_r.at[0], after)
+    arrived(cot_hbm.at[pl.ds(0, SIDE)], ends[0], halo_s.at[1], halo_r.at[1], before)
+    widen(cot, rows_of, 0, SIDE)
+    widen(cot, rows_of, TILE + SIDE, SIDE)
+    for copy in list_copies:
+        copy.wait()
+
+    def requested(k):
         zz, cc = pair(k, False)
         arrived(asked.at[0], asked_in.at[zz * 2 + cc], ask_s.at[k], ask_r.at[k],
                 {"pix_0": zz, "pix_1": cc})
-        square[pl.ds(k, 1), :] = asked_in[zz * 2 + cc]
-    square[pl.ds(15, 1), :] = asked[me]
-    requests = jnp.transpose(square[...])
-
-    def reply(h, first, last):
-        for k in range(first, last):
-            zz, cc = pair(k, False)
-            go(answers.at[h, k], answers_in.at[h, me], ans_s.at[h * 15 + k],
-               ans_r.at[h * 15 + k], {"pix_0": zz, "pix_1": cc})
-
-    answer(requests, table, 0, answers)
-    reply(0, 0, 8)
-    answer(requests, table, 8, answers)
-    reply(0, 8, 15)
-    reply(1, 0, 15)
+
+    def serve(k, source):
+        zz, cc = pair(k, False)
+        asker = zz * 2 + cc
+        mix = [mixed[pl.ds(2 * n, 2), :] for n in range(8)]
+        unroll = 16
+
+        def some(i, carry):
+            for u in range(unroll):
+                at = i * unroll + u
+                pixel = source[asker if source is wanted else cc, 0, at]
+                row = rows_of[pl.ds(pixel * 2 + 2 * SIDE, 2), :]
+                for n in range(8):
+                    row = row + rows_of[pl.ds(lists[n][0, pixel], 2), :] * mix[n]
+                formed[pl.ds(k % 2 * 2 * CAP + 2 * at, 2), :] = row
+            return carry
+
+        lax.fori_loop(0, CAP // unroll, some, 0)
+        for h in range(2):
+            half = formed[pl.ds(k % 2 * 2 * CAP + h, CAP, stride=2), :]
+            answers[h, k] = half.astype(BF16)
+
+    def reply(h, k):
+        zz, cc = pair(k, False)
+        go(answers.at[h, k], answers_in.at[h, me], ans_s.at[h * 15 + k], ans_r.at[h * 15 + k],
+           {"pix_0": zz, "pix_1": cc})
+
+    requested(14)
+    chip_copy = pltpu.make_async_copy(asked_in.at[pl.ds(2 * z, 2)], chip_wanted, chip_sem)
+    chip_copy.start()
+    chip_copy.wait()
+    serve(15, chip_wanted)
+    serve(14, chip_wanted)
+    reply(0, 14)
     for h in range(2):
         answers_in[h, me] = answers[h, 15]
+    for k in range(14):
+        requested(k)
+    want_copy = pltpu.make_async_copy(asked_in, wanted, want_sem)
+    want_copy.start()
+    want_copy.wait()
+    lag = 10
+    for k in range(14):
+        serve(k, wanted)
+        reply(0, k)
+        if k == 0:
+            reply(1, 14)
+        if k >= lag:
+            reply(1, k - lag)
+        if k == 3:
+            arrived(parts.at[far, lo], relay.at[0], rs.at[0], rr.at[0], to_left)
+            go(relay.at[0], parts_in.at[left, lo], rs.at[4], rr.at[4], to_right)
+            arrived(parts.at[far, hi], relay.at[1], rs.at[1], rr.at[1], to_right)
+            go(relay.at[1], parts_in.at[right, hi], rs.at[5], rr.at[5], to_left)
+    for k in range(14 - lag, 14):
+        reply(1, k)
+    encode(3)
 
     slots = 16 * CAP
     chosen[...] = one_hot(
@@ -376,8 +408,8 @@
     fetch(1)
     gather_start(1)
     gather_far(0)
+    core_sum(0)
     gather_near(1)
-    core_sum(0)
     gather_far(1)
     x_sum(0)
     core_sum(1)
@@ -402,15 +434,24 @@
     anywhere = pl.BlockSpec(memory_space=pl.ANY)
     core, line, wide = channels // 2, channels // 8, channels // 64
     shapes = [
+        (enc_weight.shape, BF16),
+        ((16, 128), jnp.int32),
+        ((16, 128), jnp.int32),
+        ((16, 128), F32),
+        (adjoint.shape, jnp.int32),
+        (mixing.shape, F32),
         (spectra.shape, BF16),
         ((TILE + 256, features), BF16),
-        ((TILE, features), BF16),
+        ((2 * TILE + 520, SIDE), F32),
+        ((16, SIDE), F32),
+        ((8, TILE), jnp.int32),
+        ((4 * CAP + 8, SIDE), F32),
         ((4, rows, features), BF16),
         ((4, rows, features), BF16),
         ((2, rows // 2, features), BF16),
-        ((16, 1, 128), F32),
-        ((16, 1, 128), F32),
-        ((128, 128), F32),
+        ((16, 1, 128), jnp.int32),
+        ((16, 1, 128), jnp.int32),
+        None,
         ((rows, 128), F32),
         ((2, 16, CAP, SIDE), BF16),
         ((2, 16, CAP, SIDE), BF16),
@@ -432,14 +473,18 @@
         ((2, 2, 4, 8, wide, SIDE), BF16),
         ((channels, SIDE), F32),
     ]
+    split = shapes.index(None)
     counts = [2, 15, 30, 6, 12, 2, 6, 14, 14, 48, 8]
     encoded = pl.pallas_call(
         whole_kernel,
         out_shape=jax.ShapeDtypeStruct((channels, features), BF16),
-        in_specs=[anywhere, vmem, vmem, vmem, vmem, anywhere, vmem, vmem],
+        in_specs=[anywhere] * 8,
         out_specs=vmem,
-        scratch_shapes=[pltpu.VMEM(shape, kind) for shape, kind in shapes]
-        + [dma((4,)), dma(())]
+        scratch_shapes=[pltpu.VMEM(*shape) for shape in shapes[:split]]
+        + [pltpu.SMEM((16, 1, 128), jnp.int32), pltpu.SMEM((2, 1, 128), jnp.int32)]
+        + [pltpu.SMEM((1, TILE), jnp.int32)] * 8
+        + [pltpu.VMEM(*shape) for shape in shapes[split + 1 :]]
+        + [dma((4,)), dma(()), dma((8,)), dma(()), dma(()), dma((6,))]
         + [dma((n,)) for n in counts for _ in range(2)],
         compiler_params=pltpu.CompilerParams(collective_id=0, has_side_effects=True),
         name="whole",

time: 80.1 us -> 68.7 us (0.86)
  Pallas kernels: 77.8 us -> 66.4 us
    pallas_call x1, Pallas kernels: 77.8 us -> 66.4 us  [shards(): pl.pallas_call(whole_kernel, out_shape=jax.ShapeDtypeStruct((channels, fe...]
where the time goes in v4:
time: 68.7 us; the launch traced here: 68.5 us
  Pallas kernels  66.4 us (97%)
  other arithmetic  2.16 us (3%)
    pallas_call x1, Pallas kernels, shards(): pl.pallas_call(whole_kernel, out_shape=jax.ShapeDtypeStruct((channels, fe...  66.4 us
    convert_element_type x1, other arithmetic, shards(): return encoded.astype(F32)  2.16 us

profile of v4, /device:TPU:1, one launch (start us, length us, event | category | flops | bytes accessed | tf_op | source)
XLA Modules:
  0.0 68.5 jit_solution(14367817358054337689)
XLA Ops:
  0.0 66.4 %whole.1 = bf16[1152,256]{1,0:T(8,128)(2,1)} custom-call(bf16[2048,1152]{1,0:T(8,128)(2,1)} %spec_hbm.1, bf16[1152,256]{1,0:T(8,128)(2,1)} %weight_hbm.1, s32[16,128]{1,0:T(8,128)} %bitcast.3, s32[16,128]{1,0:T(8,128)} %bitcast.4, f32[16,128]{1,0:T(8,128)} %bitcast.5, bf16[4096,256]{1,0:T(8,128)(2,1)} %cot_hbm.1, s32[8,4096]{1,0:T(8,128)} %adjoint_hbm.1, ...), custom_call_target="tpu_custom_call" | custom-call | tf_op jit(solution)/shard_map/whole/pallas_call | solution.py:478
  66.4 2.2 %convert_element_type.3 = f32[1152,256]{1,0:T(8,128)} convert(bf16[1152,256]{1,0:T(8,128)(2,1)} %whole.1) | non-fusion elementwise | flops 294912 | bytes 1769472 | tf_op jit(solution)/shard_map/convert_element_type | solution.py:501

commit v5 on v4

--- a/solution.py
+++ b/solution.py
@@ -93,8 +93,8 @@
                  wanted, chip_wanted, *rest):
     lists, rest = rest[:8], rest[8:]
     (columns, answers, answers_in, slope, chosen, part, shards, total, turned, cs, cr, mine, xs, xr,
-                 xsum, zf, zs, zr, pieces, result, load_sems, cot_sem, list_sems, want_sem,
-     chip_sem, in_sems,
+                 xsum, zf, zs, zr, pieces, result, ordered, load_sems, cot_sem, list_sems, want_sem,
+     chip_sem, in_sems, out_sems,
      halo_s, halo_r, ask_s, ask_r, ans_s, ans_r, rs, rr, gs, gr, core_s, core_r, xs_s, xs_r, zs_s,
      zs_r, pz_s, pz_r, px_s, px_r, pc_s, pc_r) = rest
     x, z, c, y = (lax.axis_index(name) for name in AXES)
@@ -112,6 +112,13 @@
         copy = send(*args)
         copy.start()
         sends.append(copy)
+
+    finished = [0]
+
+    def drain(upto):
+        for copy in sends[finished[0] : upto]:
+            copy.wait_send()
+        finished[0] = max(upto, finished[0])
 
     def arrived(*args):
         send(*args).wait_recv()
@@ -204,7 +211,7 @@
         zz, cc = pair(k, False)
         asker = zz * 2 + cc
         mix = [mixed[pl.ds(2 * n, 2), :] for n in range(8)]
-        unroll = 16
+        unroll = 32
 
         def some(i, carry):
             for u in range(unroll):
@@ -248,7 +255,7 @@
             reply(1, 14)
         if k >= lag:
             reply(1, k - lag)
-        if k == 3:
+        if k == 0:
             arrived(parts.at[far, lo], relay.at[0], rs.at[0], rr.at[0], to_left)
             go(relay.at[0], parts_in.at[left, lo], rs.at[4], rr.at[4], to_right)
             arrived(parts.at[far, hi], relay.at[1], rs.at[1], rr.at[1], to_right)
@@ -297,9 +304,9 @@
         mine_, store = part.at[h], shards.at[h]
         go(mine_.at[lo], store.at[y, lo], gs.at[i], gr.at[i], to_right)
         go(mine_.at[hi], store.at[y, hi], gs.at[i + 1], gr.at[i + 1], to_left)
+        multiply(h, part[h], y, True)
         go(mine_.at[hi], store.at[y, hi], gs.at[i + 2], gr.at[i + 2], to_right)
         go(mine_.at[lo], store.at[y, lo], gs.at[i + 3], gr.at[i + 3], to_left)
-        multiply(h, part[h], y, True)
 
     def gather_near(h):
         i = h * 6
@@ -381,6 +388,20 @@
         group = pieces.at[h, c, x]
         go(group, group, pc_s.at[h * 4], pc_r.at[h * 4], {"pix_1": o})
 
+    def assemble(h, core):
+        for xx in range(4):
+            for zz in range(8):
+                row = xx * line + zz * wide
+                result[core, pl.ds(row, wide), :] = pieces[h, core, xx, zz].astype(F32)
+        ordered[h, core] = result[core].astype(BF16)
+        target = out.at[pl.ds(pl.multiple_of(core * core_lines, 8), core_lines),
+                        pl.ds(h * SIDE, SIDE)]
+        copy = pltpu.make_async_copy(ordered.at[h, core], target, out_sems.at[len(results)])
+        copy.start()
+        results.append(copy)
+
+    results = []
+
     def x_gather(h):
         for e in near:
             column = lax.rem(x + 4 - e, 4)
@@ -390,17 +411,13 @@
                 arrived(piece, piece, px_s.at[at], px_r.at[at], {"obs": column})
             group = pieces.at[h, c, column]
             go(group, group, pc_s.at[h * 4 + e], pc_r.at[h * 4 + e], {"pix_1": o})
+        assemble(h, c)
 
     def core_gather(h):
         for e in (0,) + near:
             group = pieces.at[h, o, lax.rem(x + 4 - e, 4)]
             arrived(group, group, pc_s.at[h * 4 + e], pc_r.at[h * 4 + e], {"pix_1": o})
-        for cc in range(2):
-            for xx in range(4):
-                for zz in range(8):
-                    row = cc * core_lines + xx * line + zz * wide
-                    result[pl.ds(row, wide), :] = pieces[h, cc, xx, zz].astype(F32)
-        out[:, h * SIDE : (h + 1) * SIDE] = result[...].astype(out.dtype)
+        assemble(h, o)
 
     fetch(0)
     gather_start(0)
@@ -410,27 +427,35 @@
     gather_far(0)
     core_sum(0)
     gather_near(1)
+    gathered = len(sends)
     gather_far(1)
     x_sum(0)
     core_sum(1)
+    x_sent = len(sends)
+    drain(gathered)
     z_sum(0)
     x_sum(1)
+    z_sent = len(sends)
+    drain(x_sent)
     z_gather(0)
     z_sum(1)
+    first_sent = len(sends)
+    drain(z_sent)
     x_gather(0)
     z_gather(1)
     core_gather(0)
+    drain(first_sent)
     x_gather(1)
     core_gather(1)
-    for copy in sends:
-        copy.wait_send()
+    drain(len(sends))
+    for copy in results:
+        copy.wait()
 
 
 def shards(spectra, enc_weight, pix_tile, pix_local, foot_weight, cotangent, adjoint, mixing):
     rows, features = spectra.shape[0] // 4, cotangent.shape[1]
     channels = spectra.shape[1]
     dma = pltpu.SemaphoreType.DMA
-    vmem = pl.BlockSpec(memory_space=pltpu.VMEM)
     anywhere = pl.BlockSpec(memory_space=pl.ANY)
     core, line, wide = channels // 2, channels // 8, channels // 64
     shapes = [
@@ -471,7 +496,8 @@
         ((2, 8, wide, SIDE), BF16),
         ((2, 8, wide, SIDE), BF16),
         ((2, 2, 4, 8, wide, SIDE), BF16),
-        ((channels, SIDE), F32),
+        ((2, core, SIDE), F32),
+        ((2, 2, core, SIDE), BF16),
     ]
     split = shapes.index(None)
     counts = [2, 15, 30, 6, 12, 2, 6, 14, 14, 48, 8]
@@ -479,12 +505,12 @@
         whole_kernel,
         out_shape=jax.ShapeDtypeStruct((channels, features), BF16),
         in_specs=[anywhere] * 8,
-        out_specs=vmem,
+        out_specs=anywhere,
         scratch_shapes=[pltpu.VMEM(*shape) for shape in shapes[:split]]
         + [pltpu.SMEM((16, 1, 128), jnp.int32), pltpu.SMEM((2, 1, 128), jnp.int32)]
         + [pltpu.SMEM((1, TILE), jnp.int32)] * 8
         + [pltpu.VMEM(*shape) for shape in shapes[split + 1 :]]
-        + [dma((4,)), dma(()), dma((8,)), dma(()), dma(()), dma((6,))]
+        + [dma((4,)), dma(()), dma((8,)), dma(()), dma(()), dma((6,)), dma((4,))]
         + [dma((n,)) for n in counts for _ in range(2)],
         compiler_params=pltpu.CompilerParams(collective_id=0, has_side_effects=True),
         name="whole",

time: 68.7 us -> 68.3 us (level)
  no operation moved by 1% of the time
where the time goes in v5:
time: 68.3 us; the launch traced here: 68.2 us
  Pallas kernels  66 us (97%)
  other arithmetic  2.16 us (3%)
    pallas_call x1, Pallas kernels, shards(): pl.pallas_call(whole_kernel, out_shape=jax.ShapeDtypeStruct((channels, fe...  66 us
    convert_element_type x1, other arithmetic, shards(): return encoded.astype(F32)  2.16 us

profile of v5, /device:TPU:1, one launch (start us, length us, event | category | flops | bytes accessed | tf_op | source)
XLA Modules:
  0.0 68.2 jit_solution(8663989622269021712)
XLA Ops:
  0.0 66.0 %whole.1 = bf16[1152,256]{1,0:T(8,128)(2,1)} custom-call(bf16[2048,1152]{1,0:T(8,128)(2,1)} %spec_hbm.1, bf16[1152,256]{1,0:T(8,128)(2,1)} %weight_hbm.1, s32[16,128]{1,0:T(8,128)} %bitcast.3, s32[16,128]{1,0:T(8,128)} %bitcast.4, f32[16,128]{1,0:T(8,128)} %bitcast.5, bf16[4096,256]{1,0:T(8,128)(2,1)} %cot_hbm.1, s32[8,4096]{1,0:T(8,128)} %adjoint_hbm.1, ...), custom_call_target="tpu_custom_call" | custom-call | tf_op jit(solution)/shard_map/whole/pallas_call | solution.py:504
  66.0 2.2 %convert_element_type.3 = f32[1152,256]{1,0:T(8,128)} convert(bf16[1152,256]{1,0:T(8,128)(2,1)} %whole.1) | non-fusion elementwise | flops 294912 | bytes 1769472 | tf_op jit(solution)/shard_map/convert_element_type | solution.py:527

commit v6 on v5

--- a/solution.py
+++ b/solution.py
@@ -106,22 +106,16 @@
     lo, hi = pl.ds(0, rows // 2), pl.ds(rows // 2, rows // 2)
     near = (1, 3, 2)
     ring = (1, 7, 2, 6, 3, 5, 4)
-    sends = []
+    sibling = {"pix_1": o}
 
     def go(*args):
-        copy = send(*args)
-        copy.start()
-        sends.append(copy)
-
-    finished = [0]
-
-    def drain(upto):
-        for copy in sends[finished[0] : upto]:
-            copy.wait_send()
-        finished[0] = max(upto, finished[0])
-
-    def arrived(*args):
-        send(*args).wait_recv()
+        send(*args).start()
+
+    def landed(ref, sem):
+        send(ref, ref, sem, sem, sibling).wait_recv()
+
+    def gone(ref, sem):
+        send(ref, ref, sem, sem, sibling).wait_send()
 
     barrier, count = greet()
     operands = ((adjoint_hbm, adjoint), (tile_hbm, tile), (local_hbm, local), (foot_hbm, foot),
@@ -166,11 +160,11 @@
     pl.semaphore_wait(barrier, count)
     for k in range(15):
         zz, cc = pair(k, True)
-        go(asked.at[zz * 2 + cc], asked_in.at[me], ask_s.at[k], ask_r.at[k],
+        go(asked.at[zz * 2 + cc], asked_in.at[me], ask_s.at[0], ask_r.at[k // 14],
            {"pix_0": zz, "pix_1": cc})
     ends = cot.at[pl.ds(0, SIDE)], cot.at[pl.ds(TILE + SIDE, SIDE)]
     go(cot_hbm.at[pl.ds(0, SIDE)], ends[1], halo_s.at[0], halo_r.at[0], before)
-    go(cot_hbm.at[pl.ds(TILE - SIDE, SIDE)], ends[0], halo_s.at[1], halo_r.at[1], after)
+    go(cot_hbm.at[pl.ds(TILE - SIDE, SIDE)], ends[0], halo_s.at[0], halo_r.at[0], after)
 
     cot_copy.wait()
 
@@ -190,22 +184,16 @@
 
     encode(0)
     go(parts.at[far, lo], relay.at[0], rs.at[0], rr.at[0], to_right)
-    go(parts.at[far, hi], relay.at[1], rs.at[1], rr.at[1], to_left)
+    go(parts.at[far, hi], relay.at[1], rs.at[0], rr.at[1], to_left)
     encode(1)
-    go(parts.at[right], parts_in.at[y], rs.at[2], rr.at[2], to_right)
+    go(parts.at[right], parts_in.at[y], rs.at[0], rr.at[2], to_right)
     encode(2)
-    go(parts.at[left], parts_in.at[y], rs.at[3], rr.at[3], to_left)
-    arrived(cot_hbm.at[pl.ds(0, SIDE)], ends[1], halo_s.at[0], halo_r.at[0], after)
-    arrived(cot_hbm.at[pl.ds(0, SIDE)], ends[0], halo_s.at[1], halo_r.at[1], before)
+    go(parts.at[left], parts_in.at[y], rs.at[0], rr.at[2], to_left)
+    landed(cot.at[pl.ds(0, 2 * SIDE)], halo_r.at[0])
     widen(cot, rows_of, 0, SIDE)
     widen(cot, rows_of, TILE + SIDE, SIDE)
     for copy in list_copies:
         copy.wait()
-
-    def requested(k):
-        zz, cc = pair(k, False)
-        arrived(asked.at[0], asked_in.at[zz * 2 + cc], ask_s.at[k], ask_r.at[k],
-                {"pix_0": zz, "pix_1": cc})
 
     def serve(k, source):
         zz, cc = pair(k, False)
@@ -230,10 +218,10 @@
 
     def reply(h, k):
         zz, cc = pair(k, False)
-        go(answers.at[h, k], answers_in.at[h, me], ans_s.at[h * 15 + k], ans_r.at[h * 15 + k],
+        go(answers.at[h, k], answers_in.at[h, me], ans_s.at[h], ans_r.at[h],
            {"pix_0": zz, "pix_1": cc})
 
-    requested(14)
+    landed(asked_in.at[0], ask_r.at[1])
     chip_copy = pltpu.make_async_copy(asked_in.at[pl.ds(2 * z, 2)], chip_wanted, chip_sem)
     chip_copy.start()
     chip_copy.wait()
@@ -242,8 +230,7 @@
     reply(0, 14)
     for h in range(2):
         answers_in[h, me] = answers[h, 15]
-    for k in range(14):
-        requested(k)
+    landed(asked_in.at[pl.ds(0, 14)], ask_r.at[0])
     want_copy = pltpu.make_async_copy(asked_in, wanted, want_sem)
     want_copy.start()
     want_copy.wait()
@@ -256,10 +243,10 @@
         if k >= lag:
             reply(1, k - lag)
         if k == 0:
-            arrived(parts.at[far, lo], relay.at[0], rs.at[0], rr.at[0], to_left)
-            go(relay.at[0], parts_in.at[left, lo], rs.at[4], rr.at[4], to_right)
-            arrived(parts.at[far, hi], relay.at[1], rs.at[1], rr.at[1], to_right)
-            go(relay.at[1], parts_in.at[right, hi], rs.at[5], rr.at[5], to_left)
+            landed(relay.at[0], rr.at[0])
+            go(relay.at[0], parts_in.at[left, lo], rs.at[0], rr.at[2], to_right)
+            landed(relay.at[1], rr.at[1])
+            go(relay.at[1], parts_in.at[right, hi], rs.at[0], rr.at[2], to_left)
     for k in range(14 - lag, 14):
         reply(1, k)
     encode(3)
@@ -268,10 +255,7 @@
     chosen[...] = one_hot(
         jnp.broadcast_to(columns[:, 0:1], (rows, slots)) == iota((rows, slots), 1).astype(F32)
     )
-    arrived(parts.at[0], parts_in.at[left], rs.at[2], rr.at[2], to_left)
-    arrived(parts.at[0], parts_in.at[right], rs.at[3], rr.at[3], to_right)
-    arrived(relay.at[0], parts_in.at[far, lo], rs.at[4], rr.at[4], to_left)
-    arrived(relay.at[1], parts_in.at[far, hi], rs.at[5], rr.at[5], to_right)
+    landed(parts_in.at[pl.ds(0, 3)], rr.at[2])
     pre = parts[y].astype(F32)
     for origin in (left, right, far):
         pre = pre + parts_in[origin].astype(F32)
@@ -279,10 +263,7 @@
     slope[...] = columns[:, 1:2] * (sigma * (1.0 + pre * (1.0 - sigma)))
 
     def fetch(h):
-        for k in range(15):
-            zz, cc = pair(k, True)
-            arrived(answers.at[h, k], answers_in.at[h, zz * 2 + cc], ans_s.at[h * 15 + k],
-                    ans_r.at[h * 15 + k], {"pix_0": zz, "pix_1": cc})
+        landed(answers_in.at[h, pl.ds(0, 15)], ans_r.at[h])
         rows_in = answers_in[h].reshape(slots, SIDE)
         fetched = jnp.dot(chosen[...], rows_in, preferred_element_type=F32)
         part[h] = (slope[:, h * SIDE : (h + 1) * SIDE] * fetched).astype(BF16)
@@ -302,22 +283,22 @@
     def gather_start(h):
         i = h * 6
         mine_, store = part.at[h], shards.at[h]
-        go(mine_.at[lo], store.at[y, lo], gs.at[i], gr.at[i], to_right)
-        go(mine_.at[hi], store.at[y, hi], gs.at[i + 1], gr.at[i + 1], to_left)
+        go(mine_.at[lo], store.at[y, lo], gs.at[h], gr.at[i], to_right)
+        go(mine_.at[hi], store.at[y, hi], gs.at[h], gr.at[i + 1], to_left)
         multiply(h, part[h], y, True)
-        go(mine_.at[hi], store.at[y, hi], gs.at[i + 2], gr.at[i + 2], to_right)
-        go(mine_.at[lo], store.at[y, lo], gs.at[i + 3], gr.at[i + 3], to_left)
+        go(mine_.at[hi], store.at[y, hi], gs.at[h], gr.at[i + 2], to_right)
+        go(mine_.at[lo], store.at[y, lo], gs.at[h], gr.at[i + 3], to_left)
 
     def gather_near(h):
         i = h * 6
         mine_, store = part.at[h], shards.at[h]
-        arrived(mine_.at[lo], store.at[left, lo], gs.at[i], gr.at[i], to_left)
-        go(store.at[left, lo], store.at[left, lo], gs.at[i + 4], gr.at[i + 4], to_right)
-        arrived(mine_.at[hi], store.at[right, hi], gs.at[i + 1], gr.at[i + 1], to_right)
-        go(store.at[right, hi], store.at[right, hi], gs.at[i + 5], gr.at[i + 5], to_left)
-        arrived(mine_.at[hi], store.at[left, hi], gs.at[i + 2], gr.at[i + 2], to_left)
+        landed(store.at[left, lo], gr.at[i])
+        go(store.at[left, lo], store.at[left, lo], gs.at[h], gr.at[i + 4], to_right)
+        landed(store.at[right, hi], gr.at[i + 1])
+        go(store.at[right, hi], store.at[right, hi], gs.at[h], gr.at[i + 5], to_left)
+        landed(store.at[left, hi], gr.at[i + 2])
         multiply(h, shards[h, left], left)
-        arrived(mine_.at[lo], store.at[right, lo], gs.at[i + 3], gr.at[i + 3], to_right)
+        landed(store.at[right, lo], gr.at[i + 3])
         multiply(h, shards[h, right], right)
 
     core_lines, line, wide = mine.shape[1], xs.shape[2], zs.shape[2]
@@ -325,8 +306,8 @@
     def gather_far(h):
         i = h * 6
         store = shards.at[h]
-        arrived(store.at[far, lo], store.at[far, lo], gs.at[i + 4], gr.at[i + 4], to_left)
-        arrived(store.at[far, hi], store.at[far, hi], gs.at[i + 5], gr.at[i + 5], to_right)
+        landed(store.at[far, lo], gr.at[i + 4])
+        landed(store.at[far, hi], gr.at[i + 5])
         multiply(h, shards[h, far], far)
         for j in range(total.shape[2] // SIDE):
             block = pl.ds(j * SIDE, SIDE)
@@ -336,57 +317,50 @@
         go(cs.at[h], cr.at[h], core_s.at[h], core_r.at[h], {"pix_1": o})
 
     def core_sum(h):
-        arrived(cs.at[h], cr.at[h], core_s.at[h], core_r.at[h], {"pix_1": o})
+        landed(cr.at[h], core_r.at[h])
         ours = pl.ds(pl.multiple_of(c * core_lines, 8), core_lines)
         mine[h] = turned[h, ours, :] + cr[h].astype(F32)
         for j in range(4):
             xs[h, j] = mine[h, pl.ds(j * line, line), :].astype(BF16)
         for d in near:
             peer = lax.rem(x + d, 4)
-            at = h * 3 + d - 1
-            go(xs.at[h, peer], xr.at[h, x], xs_s.at[at], xs_r.at[at], {"obs": peer})
+            go(xs.at[h, peer], xr.at[h, x], xs_s.at[h], xs_r.at[h], {"obs": peer})
 
     def x_sum(h):
         summed = mine[h, pl.ds(pl.multiple_of(x * line, 8), line), :]
+        landed(xr.at[h, pl.ds(0, 3)], xs_r.at[h])
         for d in near:
-            origin = lax.rem(x + 4 - d, 4)
-            at = h * 3 + d - 1
-            arrived(xs.at[h, 0], xr.at[h, origin], xs_s.at[at], xs_r.at[at], {"obs": origin})
-            summed = summed + xr[h, origin].astype(F32)
+            summed = summed + xr[h, lax.rem(x + 4 - d, 4)].astype(F32)
         xsum[h] = summed
         for j in range(8):
             zf[h, j] = xsum[h, pl.ds(j * wide, wide), :]
             zs[h, j] = zf[h, j].astype(BF16)
         for d in ring:
             peer = lax.rem(z + d, 8)
-            at = h * 7 + d - 1
-            go(zs.at[h, peer], zr.at[h, z], zs_s.at[at], zs_r.at[at], {"pix_0": peer})
+            go(zs.at[h, peer], zr.at[h, z], zs_s.at[h], zs_r.at[h], {"pix_0": peer})
 
     def z_sum(h):
         own = zf[h, z]
+        landed(zr.at[h, pl.ds(0, 7)], zs_r.at[h])
         for d in ring:
-            origin = lax.rem(z + 8 - d, 8)
-            at = h * 7 + d - 1
-            arrived(zs.at[h, 0], zr.at[h, origin], zs_s.at[at], zs_r.at[at], {"pix_0": origin})
-            own = own + zr[h, origin].astype(F32)
+            own = own + zr[h, lax.rem(z + 8 - d, 8)].astype(F32)
         pieces[h, c, x, z] = own.astype(BF16)
         piece = pieces.at[h, c, x, z]
         for d in ring:
             at = h * 7 + d - 1
-            go(piece, piece, pz_s.at[at], pz_r.at[at], {"pix_0": lax.rem(z + d, 8)})
+            go(piece, piece, pz_s.at[h], pz_r.at[at], {"pix_0": lax.rem(z + d, 8)})
 
     def z_gather(h):
         for d in (0,) + ring:
             origin = lax.rem(z + 8 - d, 8)
             piece = pieces.at[h, c, x, origin]
             if d:
-                at = h * 7 + d - 1
-                arrived(piece, piece, pz_s.at[at], pz_r.at[at], {"pix_0": origin})
+                landed(piece, pz_r.at[h * 7 + d - 1])
             for e in near:
-                at = (h * 8 + d) * 3 + e - 1
-                go(piece, piece, px_s.at[at], px_r.at[at], {"obs": lax.rem(x + e, 4)})
+                at = h * 3 + e - 1
+                go(piece, piece, px_s.at[h], px_r.at[at], {"obs": lax.rem(x + e, 4)})
         group = pieces.at[h, c, x]
-        go(group, group, pc_s.at[h * 4], pc_r.at[h * 4], {"pix_1": o})
+        go(group, group, pc_s.at[h], pc_r.at[h], {"pix_1": o})
 
     def assemble(h, core):
         for xx in range(4):
@@ -405,18 +379,13 @@
     def x_gather(h):
         for e in near:
             column = lax.rem(x + 4 - e, 4)
-            for d in (0,) + ring:
-                at = (h * 8 + d) * 3 + e - 1
-                piece = pieces.at[h, c, column, lax.rem(z + 8 - d, 8)]
-                arrived(piece, piece, px_s.at[at], px_r.at[at], {"obs": column})
             group = pieces.at[h, c, column]
-            go(group, group, pc_s.at[h * 4 + e], pc_r.at[h * 4 + e], {"pix_1": o})
+            landed(group, px_r.at[h * 3 + e - 1])
+            go(group, group, pc_s.at[h], pc_r.at[h], {"pix_1": o})
         assemble(h, c)
 
     def core_gather(h):
-        for e in (0,) + near:
-            group = pieces.at[h, o, lax.rem(x + 4 - e, 4)]
-            arrived(group, group, pc_s.at[h * 4 + e], pc_r.at[h * 4 + e], {"pix_1": o})
+        landed(pieces.at[h, o], pc_r.at[h])
         assemble(h, o)
 
     fetch(0)
@@ -427,27 +396,35 @@
     gather_far(0)
     core_sum(0)
     gather_near(1)
-    gathered = len(sends)
     gather_far(1)
     x_sum(0)
     core_sum(1)
-    x_sent = len(sends)
-    drain(gathered)
+    gone(asked.at[pl.ds(0, 15)], ask_s.at[0])
+    gone(cot.at[pl.ds(0, 2 * SIDE)], halo_s.at[0])
+    gone(parts, rs.at[0])
+    for h in range(2):
+        gone(answers.at[h, pl.ds(0, 15)], ans_s.at[h])
+        gone(shards.at[h, pl.ds(0, 3)], gs.at[h])
     z_sum(0)
     x_sum(1)
-    z_sent = len(sends)
-    drain(x_sent)
+    for h in range(2):
+        gone(cs.at[h], core_s.at[h])
+        gone(xs.at[h, pl.ds(0, 3)], xs_s.at[h])
     z_gather(0)
     z_sum(1)
-    first_sent = len(sends)
-    drain(z_sent)
+    for h in range(2):
+        gone(zs.at[h, pl.ds(0, 7)], zs_s.at[h])
     x_gather(0)
     z_gather(1)
     core_gather(0)
-    drain(first_sent)
+    for h in range(2):
+        gone(pieces.at[h, 0, 0, pl.ds(0, 7)], pz_s.at[h])
+    gone(pieces.at[0, 0, pl.ds(0, 3)], px_s.at[0])
     x_gather(1)
     core_gather(1)
-    drain(len(sends))
+    gone(pieces.at[1, 0, pl.ds(0, 3)], px_s.at[1])
+    for h in range(2):
+        gone(pieces.at[h, 0], pc_s.at[h])
     for copy in results:
         copy.wait()
 
@@ -500,7 +477,7 @@
         ((2, 2, core, SIDE), BF16),
     ]
     split = shapes.index(None)
-    counts = [2, 15, 30, 6, 12, 2, 6, 14, 14, 48, 8]
+    counts = [1, 1, 1, 2, 2, 2, 1, 3, 2, 12, 2, 2, 2, 2, 2, 2, 2, 14, 2, 6, 2, 2]
     encoded = pl.pallas_call(
         whole_kernel,
         out_shape=jax.ShapeDtypeStruct((channels, features), BF16),
@@ -511,7 +488,7 @@
         + [pltpu.SMEM((1, TILE), jnp.int32)] * 8
         + [pltpu.VMEM(*shape) for shape in shapes[split + 1 :]]
         + [dma((4,)), dma(()), dma((8,)), dma(()), dma(()), dma((6,)), dma((4,))]
-        + [dma((n,)) for n in counts for _ in range(2)],
+        + [dma((n,)) for n in counts],
         compiler_params=pltpu.CompilerParams(collective_id=0, has_side_effects=True),
         name="whole",
     )(

time: 68.3 us -> 66.1 us (0.968)
  Pallas kernels: 66 us -> 63.8 us
    pallas_call x1, Pallas kernels: 66 us -> 63.8 us  [shards(): pl.pallas_call(whole_kernel, out_shape=jax.ShapeDtypeStruct((channels, fe...]
where the time goes in v6:
time: 66.1 us; the launch traced here: 65.9 us
  Pallas kernels  63.8 us (97%)
  other arithmetic  2.16 us (3%)
    pallas_call x1, Pallas kernels, shards(): pl.pallas_call(whole_kernel, out_shape=jax.ShapeDtypeStruct((channels, fe...  63.8 us
    convert_element_type x1, other arithmetic, shards(): return encoded.astype(F32)  2.16 us

profile of v6, /device:TPU:1, one launch (start us, length us, event | category | flops | bytes accessed | tf_op | source)
XLA Modules:
  0.0 65.9 jit_solution(14621999544291242065)
XLA Ops:
  0.0 63.8 %whole.1 = bf16[1152,256]{1,0:T(8,128)(2,1)} custom-call(bf16[2048,1152]{1,0:T(8,128)(2,1)} %spec_hbm.1, bf16[1152,256]{1,0:T(8,128)(2,1)} %weight_hbm.1, s32[16,128]{1,0:T(8,128)} %bitcast.3, s32[16,128]{1,0:T(8,128)} %bitcast.4, f32[16,128]{1,0:T(8,128)} %bitcast.5, bf16[4096,256]{1,0:T(8,128)(2,1)} %cot_hbm.1, s32[8,4096]{1,0:T(8,128)} %adjoint_hbm.1, ...), custom_call_target="tpu_custom_call" | custom-call | tf_op jit(solution)/shard_map/whole/pallas_call | solution.py:481
  63.8 2.2 %convert_element_type.3 = f32[1152,256]{1,0:T(8,128)} convert(bf16[1152,256]{1,0:T(8,128)(2,1)} %whole.1) | non-fusion elementwise | flops 294912 | bytes 1769472 | tf_op jit(solution)/shard_map/convert_element_type | solution.py:504

commit v7 on v6

--- a/solution.py
+++ b/solution.py
@@ -90,11 +90,11 @@
 
 def whole_kernel(spec_hbm, weight_hbm, tile_hbm, local_hbm, foot_hbm, cot_hbm, adjoint_hbm,
                  mixing_hbm, out, weight, tile, local, foot, adjoint, mixing, spec, cot, rows_of, mixed, near_rows, formed, parts, parts_in, relay, asked, asked_in,
-                 wanted, chip_wanted, *rest):
+                 wanted, chip_wanted, near_wanted, *rest):
     lists, rest = rest[:8], rest[8:]
     (columns, answers, answers_in, slope, chosen, part, shards, total, turned, cs, cr, mine, xs, xr,
                  xsum, zf, zs, zr, pieces, result, ordered, load_sems, cot_sem, list_sems, want_sem,
-     chip_sem, in_sems, out_sems,
+     chip_sem, near_sems, in_sems, out_sems,
      halo_s, halo_r, ask_s, ask_r, ans_s, ans_r, rs, rr, gs, gr, core_s, core_r, xs_s, xs_r, zs_s,
      zs_r, pz_s, pz_r, px_s, px_r, pc_s, pc_r) = rest
     x, z, c, y = (lax.axis_index(name) for name in AXES)
@@ -160,7 +160,7 @@
     pl.semaphore_wait(barrier, count)
     for k in range(15):
         zz, cc = pair(k, True)
-        go(asked.at[zz * 2 + cc], asked_in.at[me], ask_s.at[0], ask_r.at[k // 14],
+        go(asked.at[zz * 2 + cc], asked_in.at[me], ask_s.at[0], ask_r.at[(k >= 10) + (k == 14)],
            {"pix_0": zz, "pix_1": cc})
     ends = cot.at[pl.ds(0, SIDE)], cot.at[pl.ds(TILE + SIDE, SIDE)]
     go(cot_hbm.at[pl.ds(0, SIDE)], ends[1], halo_s.at[0], halo_r.at[0], before)
@@ -195,16 +195,14 @@
     for copy in list_copies:
         copy.wait()
 
-    def serve(k, source):
-        zz, cc = pair(k, False)
-        asker = zz * 2 + cc
+    def serve(k, source, slot):
         mix = [mixed[pl.ds(2 * n, 2), :] for n in range(8)]
         unroll = 32
 
         def some(i, carry):
             for u in range(unroll):
                 at = i * unroll + u
-                pixel = source[asker if source is wanted else cc, 0, at]
+                pixel = source[slot, 0, at]
                 row = rows_of[pl.ds(pixel * 2 + 2 * SIDE, 2), :]
                 for n in range(8):
                     row = row + rows_of[pl.ds(lists[n][0, pixel], 2), :] * mix[n]
@@ -221,33 +219,51 @@
         go(answers.at[h, k], answers_in.at[h, me], ans_s.at[h], ans_r.at[h],
            {"pix_0": zz, "pix_1": cc})
 
-    landed(asked_in.at[0], ask_r.at[1])
+    landed(asked_in.at[0], ask_r.at[2])
     chip_copy = pltpu.make_async_copy(asked_in.at[pl.ds(2 * z, 2)], chip_wanted, chip_sem)
     chip_copy.start()
     chip_copy.wait()
-    serve(15, chip_wanted)
-    serve(14, chip_wanted)
+    serve(15, chip_wanted, c)
+    landed(asked_in.at[pl.ds(0, 4)], ask_r.at[1])
+    near_copies = []
+    for i, d in enumerate((1, 7)):
+        rows_in = asked_in.at[pl.ds(2 * lax.rem(z + 8 - d, 8), 2)]
+        target = near_wanted.at[pl.ds(2 * i, 2)]
+        near_copies.append(pltpu.make_async_copy(rows_in, target, near_sems.at[i]))
+        near_copies[i].start()
+    serve(14, chip_wanted, o)
     reply(0, 14)
     for h in range(2):
         answers_in[h, me] = answers[h, 15]
-    landed(asked_in.at[pl.ds(0, 14)], ask_r.at[0])
-    want_copy = pltpu.make_async_copy(asked_in, wanted, want_sem)
-    want_copy.start()
-    want_copy.wait()
-    lag = 10
-    for k in range(14):
-        serve(k, wanted)
+    for copy in near_copies:
+        copy.wait()
+    served = [14]
+    lag = 15
+
+    def serve_and_reply(k, source, slot):
+        serve(k, source, slot)
         reply(0, k)
-        if k == 0:
-            reply(1, 14)
-        if k >= lag:
-            reply(1, k - lag)
-        if k == 0:
+        served.append(k)
+        if len(served) > lag:
+            reply(1, served[len(served) - lag - 1])
+
+    for k in (10, 11, 12):
+        d, e = order[k]
+        serve_and_reply(k, near_wanted, (0 if d == 1 else 2) + lax.rem(c + e, 2))
+        if k == 11:
             landed(relay.at[0], rr.at[0])
             go(relay.at[0], parts_in.at[left, lo], rs.at[0], rr.at[2], to_right)
             landed(relay.at[1], rr.at[1])
             go(relay.at[1], parts_in.at[right, hi], rs.at[0], rr.at[2], to_left)
-    for k in range(14 - lag, 14):
+    landed(asked_in.at[pl.ds(0, 10)], ask_r.at[0])
+    want_copy = pltpu.make_async_copy(asked_in, wanted, want_sem)
+    want_copy.start()
+    serve_and_reply(13, near_wanted, 2 + lax.rem(c + order[13][1], 2))
+    want_copy.wait()
+    for k in range(10):
+        zz, cc = pair(k, False)
+        serve_and_reply(k, wanted, zz * 2 + cc)
+    for k in served[-lag:]:
         reply(1, k)
     encode(3)
 
@@ -289,13 +305,17 @@
         go(mine_.at[hi], store.at[y, hi], gs.at[h], gr.at[i + 2], to_right)
         go(mine_.at[lo], store.at[y, lo], gs.at[h], gr.at[i + 3], to_left)
 
-    def gather_near(h):
+    def gather_relay(h):
         i = h * 6
-        mine_, store = part.at[h], shards.at[h]
+        store = shards.at[h]
         landed(store.at[left, lo], gr.at[i])
         go(store.at[left, lo], store.at[left, lo], gs.at[h], gr.at[i + 4], to_right)
         landed(store.at[right, hi], gr.at[i + 1])
         go(store.at[right, hi], store.at[right, hi], gs.at[h], gr.at[i + 5], to_left)
+
+    def gather_near(h):
+        i = h * 6
+        store = shards.at[h]
         landed(store.at[left, hi], gr.at[i + 2])
         multiply(h, shards[h, left], left)
         landed(store.at[right, lo], gr.at[i + 3])
@@ -390,28 +410,30 @@
 
     fetch(0)
     gather_start(0)
+    gather_relay(0)
     gather_near(0)
     fetch(1)
     gather_start(1)
     gather_far(0)
+    gather_relay(1)
     core_sum(0)
     gather_near(1)
     gather_far(1)
+    core_sum(1)
     x_sum(0)
-    core_sum(1)
     gone(asked.at[pl.ds(0, 15)], ask_s.at[0])
     gone(cot.at[pl.ds(0, 2 * SIDE)], halo_s.at[0])
     gone(parts, rs.at[0])
     for h in range(2):
         gone(answers.at[h, pl.ds(0, 15)], ans_s.at[h])
         gone(shards.at[h, pl.ds(0, 3)], gs.at[h])
+    x_sum(1)
     z_sum(0)
-    x_sum(1)
     for h in range(2):
         gone(cs.at[h], core_s.at[h])
         gone(xs.at[h, pl.ds(0, 3)], xs_s.at[h])
+    z_sum(1)
     z_gather(0)
-    z_sum(1)
     for h in range(2):
         gone(zs.at[h, pl.ds(0, 7)], zs_s.at[h])
     x_gather(0)
@@ -427,6 +449,42 @@
         gone(pieces.at[h, 0], pc_s.at[h])
     for copy in results:
         copy.wait()
+
+
+def widen_kernel(narrow, wide, held, filled, in_sems, out_sems):
+    lines = held.shape[1]
+    arriving, leaving = [], []
+    for i in range(held.shape[0]):
+        rows = pl.ds(i * lines, lines)
+        arriving.append(pltpu.make_async_copy(narrow.at[rows], held.at[i], in_sems.at[i]))
+        leaving.append(pltpu.make_async_copy(filled.at[i], wide.at[rows], out_sems.at[i]))
+        arriving[i].start()
+    for i in range(held.shape[0]):
+        arriving[i].wait()
+        filled[i] = held[i].astype(F32)
+        leaving[i].start()
+    for copy in leaving:
+        copy.wait()
+
+
+def widened(narrow):
+    rows, columns = narrow.shape
+    count = 4
+    chunk = (count, rows // count, columns)
+    anywhere = pl.BlockSpec(memory_space=pl.ANY)
+    return pl.pallas_call(
+        widen_kernel,
+        out_shape=jax.ShapeDtypeStruct(narrow.shape, F32),
+        in_specs=[anywhere],
+        out_specs=anywhere,
+        scratch_shapes=[
+            pltpu.VMEM(chunk, BF16),
+            pltpu.VMEM(chunk, F32),
+            pltpu.SemaphoreType.DMA((count,)),
+            pltpu.SemaphoreType.DMA((count,)),
+        ],
+        name="widen",
+    )(narrow)
 
 
 def shards(spectra, enc_weight, pix_tile, pix_local, foot_weight, cotangent, adjoint, mixing):
@@ -477,7 +535,7 @@
         ((2, 2, core, SIDE), BF16),
     ]
     split = shapes.index(None)
-    counts = [1, 1, 1, 2, 2, 2, 1, 3, 2, 12, 2, 2, 2, 2, 2, 2, 2, 14, 2, 6, 2, 2]
+    counts = [1, 1, 1, 3, 2, 2, 1, 3, 2, 12, 2, 2, 2, 2, 2, 2, 2, 14, 2, 6, 2, 2]
     encoded = pl.pallas_call(
         whole_kernel,
         out_shape=jax.ShapeDtypeStruct((channels, features), BF16),
@@ -485,9 +543,10 @@
         out_specs=anywhere,
         scratch_shapes=[pltpu.VMEM(*shape) for shape in shapes[:split]]
         + [pltpu.SMEM((16, 1, 128), jnp.int32), pltpu.SMEM((2, 1, 128), jnp.int32)]
+        + [pltpu.SMEM((4, 1, 128), jnp.int32)]
         + [pltpu.SMEM((1, TILE), jnp.int32)] * 8
         + [pltpu.VMEM(*shape) for shape in shapes[split + 1 :]]
-        + [dma((4,)), dma(()), dma((8,)), dma(()), dma(()), dma((6,)), dma((4,))]
+        + [dma((4,)), dma(()), dma((8,)), dma(()), dma(()), dma((2,)), dma((6,)), dma((4,))]
         + [dma((n,)) for n in counts],
         compiler_params=pltpu.CompilerParams(collective_id=0, has_side_effects=True),
         name="whole",
@@ -501,7 +560,7 @@
         adjoint,
         mixing,
     )
-    return encoded.astype(F32)
+    return widened(encoded)
 
 
 def solution(mesh):

time: 66.1 us -> 66 us (level)
  other arithmetic: 2.16 us -> 0 us
  Pallas kernels: 63.8 us -> 65.9 us
    convert_element_type x1 -> x0, other arithmetic: 2.16 us -> none  [shards(): return encoded.astype(F32)]
    pallas_call x0 -> x1, Pallas kernels: none -> 2 us  [widened(): pl.pallas_call(widen_kernel, out_shape=jax.ShapeDtypeStruct(narrow.shape,...]
where the time goes in v7:
time: 66 us; the launch traced here: 65.9 us
  Pallas kernels  65.9 us (100%)
    pallas_call x1, Pallas kernels, shards(): pl.pallas_call(whole_kernel, out_shape=jax.ShapeDtypeStruct((channels, fe...  63.9 us
    pallas_call x1, Pallas kernels, widened(): pl.pallas_call(widen_kernel, out_shape=jax.ShapeDtypeStruct(narrow.shape,...  2 us

profile of v7, /device:TPU:1, one launch (start us, length us, event | category | flops | bytes accessed | tf_op | source)
XLA Modules:
  0.0 65.9 jit_solution(3620972939255206933)
XLA Ops:
  0.0 63.9 %whole.1.narrow = bf16[1152,256]{1,0:T(8,128)(2,1)} custom-call(bf16[2048,1152]{1,0:T(8,128)(2,1)} %spec_hbm.1, bf16[1152,256]{1,0:T(8,128)(2,1)} %weight_hbm.1, s32[16,128]{1,0:T(8,128)} %bitcast.3, s32[16,128]{1,0:T(8,128)} %bitcast.4, f32[16,128]{1,0:T(8,128)} %bitcast.5, bf16[4096,256]{1,0:T(8,128)(2,1)} %cot_hbm.1, s32[8,4096]{1,0:T(8,128)} %adjoint_hbm.1, ...), custom_call_target="tpu_custom_call" | custom-call | tf_op jit(solution)/shard_map/whole/pallas_call | solution.py:539
  63.9 2.0 %widen.1 = f32[1152,256]{1,0:T(8,128)} custom-call(bf16[1152,256]{1,0:T(8,128)(2,1)} %whole.1.narrow), custom_call_target="tpu_custom_call" | custom-call | tf_op jit(solution)/shard_map/widen/pallas_call | solution.py:475

commit v8 on v7

--- a/solution.py
+++ b/solution.py
@@ -238,7 +238,7 @@
     for copy in near_copies:
         copy.wait()
     served = [14]
-    lag = 15
+    lag = 12
 
     def serve_and_reply(k, source, slot):
         serve(k, source, slot)
@@ -250,11 +250,6 @@
     for k in (10, 11, 12):
         d, e = order[k]
         serve_and_reply(k, near_wanted, (0 if d == 1 else 2) + lax.rem(c + e, 2))
-        if k == 11:
-            landed(relay.at[0], rr.at[0])
-            go(relay.at[0], parts_in.at[left, lo], rs.at[0], rr.at[2], to_right)
-            landed(relay.at[1], rr.at[1])
-            go(relay.at[1], parts_in.at[right, hi], rs.at[0], rr.at[2], to_left)
     landed(asked_in.at[pl.ds(0, 10)], ask_r.at[0])
     want_copy = pltpu.make_async_copy(asked_in, wanted, want_sem)
     want_copy.start()
@@ -263,6 +258,11 @@
     for k in range(10):
         zz, cc = pair(k, False)
         serve_and_reply(k, wanted, zz * 2 + cc)
+        if k == 0:
+            landed(relay.at[0], rr.at[0])
+            go(relay.at[0], parts_in.at[left, lo], rs.at[0], rr.at[2], to_right)
+            landed(relay.at[1], rr.at[1])
+            go(relay.at[1], parts_in.at[right, hi], rs.at[0], rr.at[2], to_left)
     for k in served[-lag:]:
         reply(1, k)
     encode(3)

time: 66 us -> 65.6 us (level)
  no operation moved by 1% of the time
where the time goes in v8:
time: 65.6 us; the launch traced here: 65.4 us
  Pallas kernels  65.4 us (100%)
    pallas_call x1, Pallas kernels, shards(): pl.pallas_call(whole_kernel, out_shape=jax.ShapeDtypeStruct((channels, fe...  63.4 us
    pallas_call x1, Pallas kernels, widened(): pl.pallas_call(widen_kernel, out_shape=jax.ShapeDtypeStruct(narrow.shape,...  2 us

profile of v8, /device:TPU:1, one launch (start us, length us, event | category | flops | bytes accessed | tf_op | source)
XLA Modules:
  0.0 65.4 jit_solution(10840495251215431744)
XLA Ops:
  0.0 63.4 %whole.1.narrow = bf16[1152,256]{1,0:T(8,128)(2,1)} custom-call(bf16[2048,1152]{1,0:T(8,128)(2,1)} %spec_hbm.1, bf16[1152,256]{1,0:T(8,128)(2,1)} %weight_hbm.1, s32[16,128]{1,0:T(8,128)} %bitcast.3, s32[16,128]{1,0:T(8,128)} %bitcast.4, f32[16,128]{1,0:T(8,128)} %bitcast.5, bf16[4096,256]{1,0:T(8,128)(2,1)} %cot_hbm.1, s32[8,4096]{1,0:T(8,128)} %adjoint_hbm.1, ...), custom_call_target="tpu_custom_call" | custom-call | tf_op jit(solution)/shard_map/whole/pallas_call | solution.py:539
  63.4 2.0 %widen.1 = f32[1152,256]{1,0:T(8,128)} custom-call(bf16[1152,256]{1,0:T(8,128)(2,1)} %whole.1.narrow), custom_call_target="tpu_custom_call" | custom-call | tf_op jit(solution)/shard_map/widen/pallas_call | solution.py:475
